TPU v7x, 256 devices: a whole 4x4x8 slice. The times are simulated.
256 devices in a mesh: wide: 32 (over z, y_lo, core), narrow: 8 (over y_hi, x).
Axes of the slice: x: 4, y: 4 (y_hi: 2, y_lo: 2; y = y_hi * 2 + y_lo), z: 8, core: 2. Of those that a mesh axis runs over, the one named last changes fastest.
Arguments:
- vol_points: float32 [3, 65536], P(None, 'wide'), may hold values from 0 to 1
- vol_adjoint: bfloat16 [48, 65536], P(None, 'wide'), may hold values from -6 to 6
- surf_points: float32 [3, 32768], P(None, ('narrow', 'wide')), may hold values from 0 to 1
- tile_mask: int32 [512, 256], P('wide', 'narrow'), may hold values 0 or 1
Outputs:
- solution: float32 [48, 32768], P(None, ('narrow', 'wide'))
- residual: float32 [48, 32768], P(None, ('narrow', 'wide'))
All inputs are finite; a program needn't handle non-finite values. No bound on the sum of `tile_mask` on one device may be relied on, other than what follows from the above.
Results may differ from a plain program's by a relative error of at most 0.0039.
Values sent between devices are 32-bit elements; how exact they have to be, the bound alone decides.
No kernel may reach another device: no remote copies, remote signals or barrier semaphores. Data moves between devices by JAX's collectives and lax.ppermute only.
A program may use at most 64 MiB of HBM per device.

v0:
```python
import math

import jax
import jax.numpy as jnp
from jax import lax
from jax.sharding import PartitionSpec as P

TILE = 128


RADIUS = 0.15
KERNEL_GAIN = 3200.0
RHS_GAIN = 28.0
LOWER_EDGE = 1.0
UPPER_EDGE = 4.0


def kernel_block(sources, targets):
    squared = jnp.zeros((sources.shape[1], targets.shape[1]), jnp.float32)
    for component in range(3):
        offset = sources[component][:, None] - targets[component][None, :]
        squared = squared + offset * offset
    scaled = jnp.sqrt(squared) / RADIUS
    remain = jnp.maximum(1.0 - scaled, 0.0)
    return remain**4 * (4.0 * scaled + 1.0)


def apply_operator(field, columns, row_coords, total_surface):
    empty = jnp.zeros((field.shape[0], row_coords.shape[1]), jnp.float32)
    piece = lax.all_gather(field, "wide", axis=1, tiled=True)
    count = piece.shape[1]
    stride = math.gcd(count, 256)

    def one_block(index, accum):
        offset = index * stride
        block_vals = lax.dynamic_slice_in_dim(piece, offset, stride, 1)
        sources = lax.dynamic_slice_in_dim(columns, offset, stride, 1)
        values = kernel_block(sources, row_coords)
        return accum + jnp.dot(
            block_vals, values, precision=lax.Precision.HIGHEST, preferred_element_type=jnp.float32
        )

    partial_rows = lax.fori_loop(0, count // stride, one_block, empty)
    mixed = lax.psum_scatter(partial_rows, "narrow", scatter_dimension=1, tiled=True)
    return field + KERNEL_GAIN / total_surface * mixed


def body(vol_points, vol_adjoint, surf_points, tile_mask):
    columns = lax.all_gather(surf_points, "wide", axis=1, tiled=True)
    row_coords = lax.all_gather(surf_points, "narrow", axis=1, tiled=True)
    span = columns.shape[1]
    volume_rows = vol_points.shape[1]
    adjoint_cols = vol_adjoint.shape[0]
    width = math.gcd(span, 256)
    total_volume = volume_rows * lax.axis_size("wide")
    total_surface = surf_points.shape[1] * lax.axis_size("wide") * lax.axis_size("narrow")

    def surface_block(index, total):
        start = index * width
        targets = lax.dynamic_slice_in_dim(columns, start, width, 1)
        mask_cols = lax.dynamic_slice_in_dim(tile_mask, start // TILE, width // TILE, 1)
        expanded = jnp.broadcast_to(
            mask_cols[:, None, :, None], (volume_rows // TILE, TILE, width // TILE, TILE)
        )
        expanded = expanded.reshape(volume_rows, width).astype(jnp.float32)
        values = (kernel_block(vol_points, targets) * expanded).astype(jnp.bfloat16)
        part = jnp.dot(vol_adjoint, values, preferred_element_type=jnp.float32)
        return lax.dynamic_update_slice_in_dim(total, part, start, 1)

    term = lax.fori_loop(
        0, span // width, surface_block, jnp.zeros((adjoint_cols, span), jnp.float32)
    )
    rhs = lax.psum_scatter(term, "wide", scatter_dimension=1, tiled=True) * (
        RHS_GAIN / math.sqrt(total_volume)
    )
    centre = (LOWER_EDGE + UPPER_EDGE) / 2.0
    half_width = (UPPER_EDGE - LOWER_EDGE) / 2.0
    sigma = centre / half_width
    rho_zero = 1.0 / sigma
    rho_one = 1.0 / (2.0 * sigma - rho_zero)
    first = rhs / centre
    near = rhs - apply_operator(first, columns, row_coords, total_surface)
    update = rho_one * rho_zero * first + 2.0 * rho_one / half_width * near
    solution = first + update
    residual = near - apply_operator(update, columns, row_coords, total_surface)
    return (solution, residual)


def solution(mesh):
    return jax.shard_map(
        body,
        mesh=mesh,
        in_specs=(
            P(None, "wide"),
            P(None, "wide"),
            P(None, ("narrow", "wide")),
            P("wide", "narrow"),
        ),
        out_specs=(P(None, ("narrow", "wide")), P(None, ("narrow", "wide"))),
        check_vma=False,
    )
```

profile of v0, /device:TPU:2, one launch (start us, length us, event | category | flops | bytes accessed | tf_op | source)
XLA Modules:
  0.0 493.9 jit_solution(16150362177685174216)
XLA Ops:
  7.2 37.6 %all_gather.12 = f32[3,4096]{1,0:T(4,128)S(1)} all-gather(f32[3,128]{1,0:T(4,128)} %param.12), channel_id=1, replica_groups=mesh['wide'=32,'narrow'=8] {'wide'}, dimensions={1}, use_global_device_ids=true | all-gather | bytes 50688 | tf_op jit(solution)/shard_map/all_gather | solution.py:49
  44.9 56.2 %while.47 = (s32[]{:T(128)}, f32[48,4096]{1,0:T(8,128)S(1)}, f32[3,2048]{1,0:T(4,128)}, f32[3,4096]{1,0:T(4,128)S(1)}, s32[16,32]{1,0:T(8,128)}, /*index=5*/bf16...) while((s32[]{:T(128)}, f32[48,4096]{1,0:T(8,128)S(1)}, ...), condition=%wide.region_1.2_spmd, body=%wide.region_0.1_spmd.sunk | while | flops 59768888 | bytes 5408598 | solution.py:70
  45.0 0.8 dynamic-slice_convert_fusion.2
  46.6 1.9 fusion.91
  48.5 0.8 dynamic-slice_convert_fusion.2
  50.1 1.9 fusion.91
  52.0 0.8 dynamic-slice_convert_fusion.2
  53.6 1.9 fusion.91
  57.1 1.9 fusion.91
  59.0 0.8 dynamic-slice_convert_fusion.2
  60.6 1.9 fusion.91
  64.1 1.9 fusion.91
  67.6 1.9 fusion.91
  71.1 1.9 fusion.91
  74.6 1.9 fusion.91
  78.2 1.9 fusion.91
  81.7 1.9 fusion.91
  85.2 1.9 fusion.91
  88.7 1.9 fusion.91
  92.2 1.9 fusion.91
  95.7 1.9 fusion.91
  99.2 1.9 fusion.91
  101.1 0.9 copy-done
  102.1 29.9 %all_gather.14 = f32[3,1024]{1,0:T(4,128)S(1)} all-gather(f32[3,128]{1,0:T(4,128)S(1)} %copy-done.6), channel_id=1, replica_groups=mesh['wide'=32,'narrow'=8] {'narrow'}, dimensions={1}, use_global_device_ids=true | all-gather | bytes 13824 | tf_op jit(solution)/shard_map/all_gather | solution.py:50
  131.9 85.6 %reduce-scatter.4.cloned.1.call-done = f32[48,128]{1,0:T(8,128)} async-done(((f32[48,4096]{1,0:T(8,128)}), f32[48,128]{1,0:T(8,128)}) %reduce-scatter.4.cloned.1.call-update) | async-done | bytes 24592 | tf_op jit(solution)/shard_map/reduce_scatter | solution.py:73
  218.3 32.5 %all_gather.13 = f32[48,4096]{1,0:T(8,128)S(1)} all-gather(f32[48,128]{1,0:T(8,128)S(1)} %broadcast_multiply_fusion), channel_id=1, replica_groups=mesh['wide'=32,'narrow'=8] {'wide'}, dimensions={1}, use_global_device_ids=true | all-gather | bytes 811008 | tf_op jit(solution)/shard_map/all_gather | solution.py:30
  250.8 27.7 %while.48 = (s32[]{:T(128)}, f32[48,1024]{1,0:T(8,128)S(1)}, f32[48,4096]{1,0:T(8,128)S(1)}, f32[3,4096]{1,0:T(4,128)S(1)}, f32[3,1024]{1,0:T(4,128)S(1)}, /*ind...) while((s32[]{:T(128)}, f32[48,1024]{1,0:T(8,128)S(1)}, ...), condition=%wide.region_4.5_spmd.clone, body=%wide.region_3.4_spmd.clone.sunk | while | flops 155287552 | bytes 488653 | solution.py:43
  250.9 1.6 convolution_add_fusion.4
  252.6 1.6 convolution_add_fusion.4
  254.4 1.6 convolution_add_fusion.4
  256.1 1.6 convolution_add_fusion.4
  257.8 1.6 convolution_add_fusion.4
  259.6 1.6 convolution_add_fusion.4
  261.3 1.6 convolution_add_fusion.4
  263.0 1.6 convolution_add_fusion.4
  264.8 1.6 convolution_add_fusion.4
  266.5 1.6 convolution_add_fusion.4
  268.2 1.6 convolution_add_fusion.4
  270.0 1.6 convolution_add_fusion.4
  271.7 1.6 convolution_add_fusion.4
  273.4 1.6 convolution_add_fusion.4
  275.2 1.6 convolution_add_fusion.4
  276.9 1.6 convolution_add_fusion.4
  279.3 71.6 %reduce-scatter.6.cloned.1.call-done = f32[48,128]{1,0:T(8,128)} async-done(((f32[48,1024]{1,0:T(8,128)}), f32[48,128]{1,0:T(8,128)}) %reduce-scatter.6.cloned.1.call-update) | async-done | bytes 24592 | tf_op jit(solution)/shard_map/reduce_scatter | solution.py:44
  351.7 35.8 %all_gather.15 = f32[48,4096]{1,0:T(8,128)S(1)} all-gather(f32[48,128]{1,0:T(8,128)S(1)} %multiply_add_fusion), channel_id=1, replica_groups=mesh['wide'=32,'narrow'=8] {'wide'}, dimensions={1}, use_global_device_ids=true | all-gather | bytes 811008 | tf_op jit(solution)/shard_map/all_gather | solution.py:30
  387.5 27.7 %while.49 = (s32[]{:T(128)}, f32[48,1024]{1,0:T(8,128)S(1)}, f32[48,4096]{1,0:T(8,128)S(1)}, f32[3,4096]{1,0:T(4,128)S(1)}, f32[3,1024]{1,0:T(4,128)S(1)}, /*ind...) while((s32[]{:T(128)}, f32[48,1024]{1,0:T(8,128)S(1)}, ...), condition=%wide.region_7.8_spmd.clone, body=%wide.region_6.7_spmd.clone.sunk | while | flops 155287552 | bytes 488653 | solution.py:43
  387.6 1.6 convolution_add_fusion.5
  389.3 1.6 convolution_add_fusion.5
  391.0 1.6 convolution_add_fusion.5
  392.8 1.6 convolution_add_fusion.5
  394.5 1.6 convolution_add_fusion.5
  396.2 1.6 convolution_add_fusion.5
  398.0 1.6 convolution_add_fusion.5
  399.7 1.6 convolution_add_fusion.5
  401.4 1.6 convolution_add_fusion.5
  403.2 1.6 convolution_add_fusion.5
  404.9 1.6 convolution_add_fusion.5
  406.6 1.6 convolution_add_fusion.5
  408.4 1.6 convolution_add_fusion.5
  410.1 1.6 convolution_add_fusion.5
  411.8 1.6 convolution_add_fusion.5
  413.6 1.6 convolution_add_fusion.5
  415.9 70.1 %reduce-scatter.8.cloned.1.call-done = f32[48,128]{1,0:T(8,128)} async-done(((f32[48,1024]{1,0:T(8,128)}), f32[48,128]{1,0:T(8,128)}) %reduce-scatter.8.cloned.1.call-update) | async-done | bytes 24592 | tf_op jit(solution)/shard_map/reduce_scatter | solution.py:44
  486.0 1.4 add_subtract_fusion
  (210 shorter events, 27.4 us)
Async XLA Ops:
  7.2 210.4 %reduce-scatter.4.cloned.1.call-start = ((), (), s32[]{:S(2)}) async-start(), calls=%async_computation.3 | async-start | bytes 811008 | tf_op jit(solution)/shard_map/reduce_scatter | solution.py:73
  44.9 57.2 %copy-start.6 = (f32[3,128]{1,0:T(4,128)S(1)}, f32[3,128]{1,0:T(4,128)}, u32[]{:S(2)}) copy-start(f32[3,128]{1,0:T(4,128)} %param.12) | copy-start | bytes 4612
  44.9 1.6 copy-start.1
  44.9 1.6 copy-start.7
  48.4 1.6 copy-start.1
  48.5 1.6 copy-start.7
  51.9 1.6 copy-start.1
  52.0 1.6 copy-start.7
  55.5 1.6 copy-start.1
  55.5 1.6 copy-start.7
  59.0 1.6 copy-start.1
  59.0 1.6 copy-start.7
  62.5 1.6 copy-start.1
  62.5 1.6 copy-start.7
  66.0 1.6 copy-start.1
  66.0 1.6 copy-start.7
  69.5 1.6 copy-start.1
  69.5 1.6 copy-start.7
  73.0 1.6 copy-start.1
  73.0 1.6 copy-start.7
  76.5 1.6 copy-start.1
  76.5 1.6 copy-start.7
  80.0 1.6 copy-start.1
  80.0 1.6 copy-start.7
  83.5 1.6 copy-start.1
  83.6 1.6 copy-start.7
  87.1 1.6 copy-start.1
  87.1 1.6 copy-start.7
  90.6 1.6 copy-start.1
  90.6 1.6 copy-start.7
  94.1 1.6 copy-start.1
  94.1 1.6 copy-start.7
  97.6 1.6 copy-start.1
  97.6 1.6 copy-start.7
  101.1 0.9 copy-start
  102.0 248.9 %reduce-scatter.6.cloned.1.call-start = ((), (), s32[]{:S(2)}) async-start(), calls=%async_computation.4 | async-start | bytes 221184 | tf_op jit(solution)/shard_map/reduce_scatter | solution.py:44
  250.8 100.1 %copy-start.2 = (f32[48,128]{1,0:T(8,128)S(1)}, f32[48,128]{1,0:T(8,128)}, u32[]{:S(2)}) copy-start(f32[48,128]{1,0:T(8,128)} %reduce-scatter.4.cloned.1.call-done) | copy-start | bytes 73732
  278.5 0.7 copy-start.3
  279.2 206.8 %reduce-scatter.8.cloned.1.call-start = ((), (), s32[]{:S(2)}) async-start(), calls=%async_computation.5 | async-start | bytes 221184 | tf_op jit(solution)/shard_map/reduce_scatter | solution.py:44
  387.5 98.5 %copy-start.5 = (f32[48,128]{1,0:T(8,128)S(1)}, f32[48,128]{1,0:T(8,128)}, u32[]{:S(2)}) copy-start(f32[48,128]{1,0:T(8,128)} %reduce-scatter.6.cloned.1.call-done) | copy-start | bytes 73732
  415.2 0.7 copy-start.4
Sparse Core Ops, SparseCore 0:
  102.1 115.3 reduce-scatter.3
  279.4 71.5 reduce-scatter.5
  416.0 69.9 reduce-scatter.7
where the time goes:
time: 495 us; the launch traced here: 494 us
  waiting for transfers between devices  227 us (46%)
  blocking collectives  136 us (27%)
  matrix products  81.2 us (16%)
  local copies, waits for them, and re-layouts  16.7 us (3%)
  other arithmetic  16.1 us (3%)
  between operations  13.8 us (3%)
    reduce_scatter x2, waiting for transfers between devices, apply_operator(): lax.psum_scatter(partial_rows, 'narrow', scatter_dimension=1, tiled=True)  142 us
    reduce_scatter x1, waiting for transfers between devices, body(): lax.psum_scatter(term, 'wide', scatter_dimension=1, tiled=True)  85.6 us
    all_gather x2, blocking collectives, apply_operator(): piece = lax.all_gather(field, 'wide', axis=1, tiled=True)  68.4 us
    dot_general x32, matrix products, one_block(): jnp.dot(block_vals, values, precision=lax.Precision.HIGHEST, preferred_el...  51.3 us
    all_gather x1, blocking collectives, body(): columns = lax.all_gather(surf_points, 'wide', axis=1, tiled=True)  37.6 us
    all_gather x1, blocking collectives, body(): row_coords = lax.all_gather(surf_points, 'narrow', axis=1, tiled=True)  29.9 us
    dot_general x16, matrix products, surface_block(): part = jnp.dot(vol_adjoint, values, preferred_element_type=jnp.float32)  29.8 us
    convert_element_type x16, other arithmetic, surface_block(): expanded = expanded.reshape(volume_rows, width).astype(jnp.float32)  13.2 us
  transfers between devices with their start and end apart: 3, of which 3 were waited for; matrix products, arithmetic and copies ran while one was open for 0% of the time, Pallas kernels for 0%

commit v1 on v0

v1 whole, which is shorter than its diff:
```python
import functools
import math

import jax
import jax.numpy as jnp
from jax import lax
from jax.experimental import pallas as pl
from jax.experimental.pallas import tpu as pltpu
from jax.sharding import PartitionSpec as P

TILE = 128
RADIUS = 0.15
KERNEL_GAIN = 3200.0
RHS_GAIN = 28.0
LOWER_EDGE = 1.0
UPPER_EDGE = 4.0

SCALE = 4.0 / RADIUS
PHI = 1.0 / 256.0
FAR = 4096.0
DEPTH = 128


def split3(x):
    one = x.astype(jnp.bfloat16).astype(jnp.float32)
    rest = x - one
    two = rest.astype(jnp.bfloat16).astype(jnp.float32)
    return one, two, rest - two


def features(points, target, extra=None):
    count = points.shape[1]
    centred = (points - 0.5) * SCALE
    norm = jnp.sum(centred * centred, axis=0, keepdims=True)
    n1, n2, n3 = split3(jnp.broadcast_to(norm, (8, count)))
    row = lax.broadcasted_iota(jnp.int32, (8, count), 0)
    one, zero = jnp.ones_like(n1), jnp.zeros_like(n1)
    if target:
        c1, c2, c3 = split3(-2.0 * centred)
        tail = jnp.where(row < 3, one, jnp.where(row == 3, n1, jnp.where(row == 4, n2, jnp.where(row == 5, n3, zero))))
        groups = [c1, c2, c1, c2, c3, c1, tail]
    else:
        c1, c2, c3 = split3(centred)
        tail = jnp.where(row == 0, n1, jnp.where(row == 1, n2, jnp.where(row == 2, n3, jnp.where(row < 6, one, zero))))
        groups = [c1, c1, c2, c2, c1, c3, tail]
    used = 8 * len(groups)
    if extra is not None:
        groups.append(extra)
        used += extra.shape[0]
    groups.append(jnp.zeros((DEPTH - used, count), jnp.float32))
    return jnp.concatenate(groups, axis=0)


def profile(d2):
    d2 = jnp.maximum(d2, 1e-12)
    w = jnp.maximum(4.0 - d2 * lax.rsqrt(d2), 0.0)
    square = w * w
    return (square * square) * (5.0 - w)


def coupling_kernel(spot_ref, vol_ref, adj_ref, mask_ref, cols_ref, keep_ref, send_ref, feat_ref):
    rows = vol_ref.shape[1]
    tiles = rows // TILE
    width = cols_ref.shape[2]

    @pl.when(pl.program_id(0) == 0)
    def _():
        tile = lax.broadcasted_iota(jnp.int32, (tiles, rows), 0)
        place = lax.broadcasted_iota(jnp.int32, (tiles, rows), 1) // TILE
        onehot = jnp.where(tile == place, 1.0, 0.0)
        feat_ref[...] = features(vol_ref[...], False, onehot).T.astype(jnp.bfloat16)

    cols_tiles = mask_ref.shape[1]
    tile = lax.broadcasted_iota(jnp.int32, (cols_tiles, width), 0)
    piece = lax.broadcasted_iota(jnp.int32, (cols_tiles, width), 1) // TILE
    swapped = (piece % 2) * 2 + piece // 2
    owner = 4 * pl.program_id(0) + (swapped ^ spot_ref[0])
    pick = jnp.where(tile == owner, 1.0, 0.0).astype(jnp.bfloat16)
    absent = (1 - mask_ref[...]).astype(jnp.float32).astype(jnp.bfloat16)
    barred = FAR * jnp.dot(absent, pick, preferred_element_type=jnp.float32)
    target = features(cols_ref[0], True, barred).astype(jnp.bfloat16)

    total = jnp.zeros((adj_ref.shape[0], width), jnp.float32)
    step = 256
    for start in range(0, rows, step):
        d2 = jnp.dot(feat_ref[start:start + step, :], target, preferred_element_type=jnp.float32)
        values = profile(d2).astype(jnp.bfloat16)
        total += jnp.dot(adj_ref[:, start:start + step], values, preferred_element_type=jnp.float32)
    half = width // 2
    keep_ref[0] = total[:, :half]
    send_ref[0] = total[:, half:]


def coupling(spot, vol, adj, mask, cols):
    blocks, _, width = cols.shape
    objs = adj.shape[0]
    whole = lambda shape: pl.BlockSpec(shape, lambda z, s: (0,) * len(shape))
    out = jax.ShapeDtypeStruct((blocks, objs, width // 2), jnp.float32)
    return pl.pallas_call(
        coupling_kernel,
        grid_spec=pltpu.PrefetchScalarGridSpec(
            num_scalar_prefetch=1,
            grid=(blocks,),
            in_specs=[
                whole(vol.shape),
                whole(adj.shape),
                whole(mask.shape),
                pl.BlockSpec((1, 8, width), lambda z, s: (z, 0, 0)),
            ],
            out_specs=[pl.BlockSpec((1, objs, width // 2), lambda z, s: (z, 0, 0))] * 2,
            scratch_shapes=[pltpu.VMEM((vol.shape[1], DEPTH), jnp.bfloat16)],
        ),
        out_shape=(out, out),
        name="coupling",
        cost_estimate=pl.CostEstimate(flops=20 * vol.shape[1] * blocks * width, bytes_accessed=2 << 20, transcendentals=0),
    )(spot, vol, adj, mask, cols)


def gram_kernel(cols_ref, rows_ref, out_ref, feat_ref):
    @pl.when(pl.program_id(0) == 0)
    def _():
        for j in range(rows_ref.shape[0]):
            feat_ref[:, j * TILE:(j + 1) * TILE] = features(rows_ref[j], True).astype(jnp.bfloat16)

    source = features(cols_ref[0], False).T.astype(jnp.bfloat16)
    width = out_ref.shape[2]
    step = 256
    for start in range(0, width, step):
        d2 = jnp.dot(source, feat_ref[:, start:start + step], preferred_element_type=jnp.float32)
        out_ref[0, :, start:start + step] = profile(d2).astype(jnp.bfloat16)


def gram(cols, rows):
    blocks, _, depth = cols.shape
    width = rows.shape[0] * rows.shape[2]
    return pl.pallas_call(
        gram_kernel,
        grid=(blocks,),
        in_specs=[
            pl.BlockSpec((1, 8, depth), lambda z: (z, 0, 0)),
            pl.BlockSpec(rows.shape, lambda z: (0, 0, 0)),
        ],
        out_specs=pl.BlockSpec((1, depth, width), lambda z: (z, 0, 0)),
        out_shape=jax.ShapeDtypeStruct((blocks, depth, width), jnp.bfloat16),
        scratch_shapes=[pltpu.VMEM((DEPTH, width), jnp.bfloat16)],
        name="gram",
        cost_estimate=pl.CostEstimate(flops=20 * blocks * depth * width, bytes_accessed=8 << 20, transcendentals=0),
    )(cols, rows)


def mix_kernel(keep_ref, send_ref, gram_ref, out_ref):
    blocks, objs, half = keep_ref.shape
    width = gram_ref.shape[2]
    total = jnp.zeros((2 * objs, width), jnp.float32)
    for z in range(blocks):
        for side, ref in enumerate((keep_ref, send_ref)):
            field = ref[z]
            high = field.astype(jnp.bfloat16).astype(jnp.float32)
            both = jnp.concatenate([high, field - high], axis=0).astype(jnp.bfloat16)
            values = gram_ref[z, side * half:(side + 1) * half, :]
            total += jnp.dot(both, values, preferred_element_type=jnp.float32)
    for j in range(out_ref.shape[0]):
        out_ref[j] = total[:objs, j * TILE:(j + 1) * TILE] + total[objs:, j * TILE:(j + 1) * TILE]


def mix(keep, send, block):
    blocks, objs, half = keep.shape
    _, depth, width = block.shape
    parts = width // TILE
    return pl.pallas_call(
        mix_kernel,
        in_specs=[pl.BlockSpec(memory_space=pltpu.VMEM)] * 3,
        out_specs=pl.BlockSpec(memory_space=pltpu.VMEM),
        out_shape=jax.ShapeDtypeStruct((parts, objs, TILE), jnp.float32),
        name="mix",
        cost_estimate=pl.CostEstimate(flops=4 * objs * blocks * depth * width, bytes_accessed=10 << 20, transcendentals=0),
    )(keep, send, block)


def body(n_wide, n_narrow, vol_points, vol_adjoint, surf_points, tile_mask):
    far = n_wide // 4
    groups = [[4 * z + r for z in range(far)] for r in range(4)]
    flip = lambda x, bit: lax.ppermute(x, "wide", [(i, i ^ bit) for i in range(n_wide)])
    exchange = lambda x: lax.all_to_all(x, "wide", 0, 0, axis_index_groups=groups, tiled=True)

    def spread(x):
        pair = jnp.concatenate([x, flip(x, 2)], axis=1)
        mine = exchange(jnp.broadcast_to(pair[None], (far,) + pair.shape))
        return mine, flip(mine, 1)

    pad = lambda p: jnp.pad(p, ((0, 5), (0, 0)), constant_values=0.5)
    own = pad(surf_points)
    near_cols, other_cols = spread(own)
    cols = jnp.concatenate([near_cols, other_cols], axis=2)
    rows = own[None]
    for bit in (4, 2, 1):
        rows = jnp.concatenate([rows, lax.ppermute(rows, "narrow", [(i, i ^ bit) for i in range(n_narrow)])], axis=0)
    order = [0]
    for bit in (4, 2, 1):
        order = order + [o ^ bit for o in order]
    spot = (lax.axis_index("wide") % 4).astype(jnp.int32).reshape(1)
    where = lax.axis_index("narrow")
    rows = jnp.stack([rows[order.index(j)] for j in range(n_narrow)], axis=0)
    wanted = jnp.arange(n_narrow, dtype=jnp.int32) ^ where
    rows = sort_rows(rows, wanted)

    keep, send = coupling(spot, pad(vol_points), vol_adjoint, tile_mask, cols)
    got = flip(send, 1)
    block = gram(cols, rows)
    summed = jnp.sum(exchange(keep + got), axis=0)
    both = summed + jnp.concatenate([x for x in halves(flip(summed, 2))], axis=1)
    total_volume = vol_points.shape[1] * n_wide
    total_surface = surf_points.shape[1] * n_wide * n_narrow
    centre = (LOWER_EDGE + UPPER_EDGE) / 2.0
    half_width = (UPPER_EDGE - LOWER_EDGE) / 2.0
    sigma = centre / half_width
    rho_zero = 1.0 / sigma
    rho_one = 1.0 / (2.0 * sigma - rho_zero)
    gain = KERNEL_GAIN / total_surface * PHI

    pair_rhs = both * (RHS_GAIN / math.sqrt(total_volume) * PHI)
    pair_first = pair_rhs / centre
    mine = exchange(jnp.broadcast_to(pair_first[None], (far,) + pair_first.shape))
    mixed = mix(mine, flip(mine, 1), block)
    collect = lambda m: jnp.sum(lax.all_to_all(m, "narrow", 0, 0, tiled=True), axis=0)
    rhs, first = pair_rhs[:, :TILE], pair_first[:, :TILE]
    near = rhs - (first + gain * collect(mixed))
    update = rho_one * rho_zero * first + 2.0 * rho_one / half_width * near
    solution = first + update
    mixed = mix(*spread(update), block)
    residual = near - (update + gain * collect(mixed))
    return (solution, residual)


def halves(x):
    return x[:, TILE:], x[:, :TILE]


def sort_kernel(wanted_ref, in_ref, out_ref):
    out_ref[...] = in_ref[...]


def sort_rows(rows, wanted):
    return pl.pallas_call(
        sort_kernel,
        grid_spec=pltpu.PrefetchScalarGridSpec(
            num_scalar_prefetch=1,
            grid=(rows.shape[0],),
            in_specs=[pl.BlockSpec((1,) + rows.shape[1:], lambda j, w: (w[j], 0, 0))],
            out_specs=pl.BlockSpec((1,) + rows.shape[1:], lambda j, w: (j, 0, 0)),
        ),
        out_shape=jax.ShapeDtypeStruct(rows.shape, rows.dtype),
        name="sort_rows",
    )(wanted, rows)


def solution(mesh):
    return jax.shard_map(
        functools.partial(body, mesh.shape["wide"], mesh.shape["narrow"]),
        mesh=mesh,
        in_specs=(
            P(None, "wide"),
            P(None, "wide"),
            P(None, ("narrow", "wide")),
            P("wide", "narrow"),
        ),
        out_specs=(P(None, ("narrow", "wide")), P(None, ("narrow", "wide"))),
        check_vma=False,
    )
```

time: 495 us -> 171 us (0.35)
  waiting for transfers between devices: 227 us -> 41.3 us
  blocking collectives: 136 us -> 42.3 us
  matrix products: 81.2 us -> 0 us
  Pallas kernels: 0 us -> 49.2 us
  starting transfers between devices: 0.12 us -> 25.4 us
  between operations: 13.8 us -> 0.75 us
  other arithmetic: 16.1 us -> 3.63 us
  local copies, waits for them, and re-layouts: 16.7 us -> 7.13 us
    reduce_scatter x3 -> x0, waiting for transfers between devices: 227 us -> none  [the longest x2 142 us: apply_operator(): lax.psum_scatter(partial_rows, 'narrow', scatter_dimension=1, tiled=True)]
    all_gather x4 -> x0, blocking collectives: 136 us -> none  [the longest x2 68.4 us: apply_operator(): piece = lax.all_gather(field, 'wide', axis=1, tiled=True)]
    dot_general x48 -> x0, matrix products: 81.2 us -> none  [the longest x32 51.3 us: one_block(): jnp.dot(block_vals, values, precision=lax.Precision.HIGHEST, preferred_el...]
    pallas_call x0 -> x5, Pallas kernels: none -> 49.2 us  [the longest x1 23.4 us: coupling(): pl.pallas_call(coupling_kernel, grid_spec=pltpu.PrefetchScalarGridSpec(nu...]
    all_to_all x0 -> x3, blocking collectives: none -> 42.3 us  [the longest x2 26.9 us: body(): lax.all_to_all(m, 'narrow', 0, 0, tiled=True)]
    all_to_all x0 -> x3, waiting for transfers between devices: none -> 24.7 us  [body(): lax.all_to_all(x, 'wide', 0, 0, axis_index_groups=groups, tiled=True)]
    ppermute x0 -> x10, waiting for transfers between devices: none -> 16.7 us  [the longest x7 12.4 us: body(): lax.ppermute(x, 'wide', [(i, i ^ bit) for i in range(n_wide)])]
    all_to_all x0 -> x3, starting transfers between devices: none -> 15.4 us  [body(): lax.all_to_all(x, 'wide', 0, 0, axis_index_groups=groups, tiled=True)]
  transfers between devices with their start and end apart: 3 -> 13, of which waited for: 3 -> 11; matrix products, arithmetic and copies ran while one was open for 0% -> 2% of each run, Pallas kernels for 0% -> 8%
where the time goes in v1:
time: 171 us; the launch traced here: 170 us
  Pallas kernels  49.2 us (29%)
  blocking collectives  42.3 us (25%)
  waiting for transfers between devices  41.3 us (24%)
  starting transfers between devices  25.4 us (15%)
  local copies, waits for them, and re-layouts  7.13 us (4%)
  other arithmetic  3.63 us (2%)
    all_to_all x2, blocking collectives, body(): lax.all_to_all(m, 'narrow', 0, 0, tiled=True)  26.9 us
    all_to_all x3, waiting for transfers between devices, body(): lax.all_to_all(x, 'wide', 0, 0, axis_index_groups=groups, tiled=True)  24.7 us
    pallas_call x1, Pallas kernels, coupling(): pl.pallas_call(coupling_kernel, grid_spec=pltpu.PrefetchScalarGridSpec(nu...  23.4 us
    all_to_all x1, blocking collectives, body(): lax.all_to_all(x, 'wide', 0, 0, axis_index_groups=groups, tiled=True)  15.4 us
    all_to_all x3, starting transfers between devices, body(): lax.all_to_all(x, 'wide', 0, 0, axis_index_groups=groups, tiled=True)  15.4 us
    ppermute x7, waiting for transfers between devices, body(): lax.ppermute(x, 'wide', [(i, i ^ bit) for i in range(n_wide)])  12.4 us
    pallas_call x2, Pallas kernels, mix(): pl.pallas_call(mix_kernel, in_specs=[pl.BlockSpec(memory_space=pltpu.VMEM...  11.6 us
    pallas_call x1, Pallas kernels, gram(): pl.pallas_call(gram_kernel, grid=(blocks,), in_specs=[pl.BlockSpec((1, 8,...  9.61 us
  transfers between devices with their start and end apart: 13, of which 11 were waited for; matrix products, arithmetic and copies ran while one was open for 2% of the time, Pallas kernels for 8%

profile of v1, /device:TPU:2, one launch (start us, length us, event | category | flops | bytes accessed | tf_op | source)
XLA Modules:
  0.0 169.8 jit_solution(9237889989788958087)
XLA Ops:
  0.6 0.7 pad_bitcast_fusion
  1.3 1.6 collective-permute-start
  2.9 2.0 %collective-permute-done = f32[8,128]{1,0:T(8,128)S(1)} collective-permute-done((f32[8,128]{1,0:T(8,128)S(1)}, f32[8,128]{1,0:T(8,128)S(1)}, u32[]{:S(2)}, u32[]{:S(2)}) %collective-permute-start) | collective-permute-done | bytes 4128 | tf_op jit(solution)/shard_map/ppermute | solution.py:183
  4.9 0.6 broadcast_in_dim.8
  5.6 8.5 %all-to-all-start = ((f32[8,8,256]{2,1,0:T(8,128)}), f32[8,8,256]{2,1,0:T(8,128)S(1)}, u32[]{:S(2)}, u32[]{:S(2)}) async-start(f32[8,8,256]{2,1,0:T(8,128)} %broadcast_in_dim.8), calls=%async_computation | async-start | bytes 131072 | tf_op jit(solution)/shard_map/all_to_all | solution.py:184
  14.0 1.4 pad.8.vol_ref
  15.4 7.0 %all-to-all-done = f32[8,8,256]{2,1,0:T(8,128)S(1)} async-done(((f32[8,8,256]{2,1,0:T(8,128)}), f32[8,8,256]{2,1,0:T(8,128)S(1)}, u32[]{:S(2)}, u32[]{:S(2)}) %all-to-all-start) | async-done | bytes 65568 | tf_op jit(solution)/shard_map/all_to_all | solution.py:184
  22.4 0.0 collective-permute-start.1
  22.4 1.2 collective-permute-done.1
  23.7 0.0 copy-start.4
  23.7 0.6 copy-done.4
  24.3 23.4 %coupling.1 = (f32[8,48,256]{2,1,0:T(8,128)}, f32[8,48,256]{2,1,0:T(8,128)}) custom-call(s32[1]{0:T(128)} %bitcast.spot_ref, f32[8,2048]{1,0:T(8,128)} %pad.8.vol_ref, bf16[48,2048]{1,0:T(8,128)(2,1)} %adj_ref.1, s32[16,32]{1,0:T(8,128)} %mask_ref.1, f32[8,8,512]{2,1,0:T(8,128)} %copy-done.4), custom_call_target="tpu_custom_call" | custom-call | flops 167772160 | bytes 2097152 | tf_op jit(solution)/shard_map/coupling/pallas_call | solution.py:99
  47.8 0.1 collective-permute-start.2
  47.9 1.8 %collective-permute-done.2 = f32[8,48,256]{2,1,0:T(8,128)S(1)} collective-permute-done((f32[8,48,256]{2,1,0:T(8,128)}, f32[8,48,256]{2,1,0:T(8,128)S(1)}, u32[]{:S(2)}, u32[]{:S(2)}) %collective-permute-start.2) | collective-permute-done | bytes 393248 | tf_op jit(solution)/shard_map/ppermute | solution.py:183
  49.7 1.8 %add.31 = f32[8,48,256]{2,1,0:T(8,128)} add(f32[8,48,256]{2,1,0:T(8,128)} %get-tuple-element.4, f32[8,48,256]{2,1,0:T(8,128)S(1)} %collective-permute-done.2) | non-fusion elementwise | flops 98304 | bytes 1179648 | tf_op jit(solution)/shard_map/add | solution.py:210
  51.5 3.5 %all-to-all-start.1 = ((f32[8,48,256]{2,1,0:T(8,128)}), f32[8,48,256]{2,1,0:T(8,128)S(1)}, u32[]{:S(2)}, u32[]{:S(2)}) async-start(f32[8,48,256]{2,1,0:T(8,128)} %add.31), calls=%async_computation.1 | async-start | bytes 786432 | tf_op jit(solution)/shard_map/all_to_all | solution.py:184
  55.0 3.3 %collective-permute-start.5 = (f32[1,8,128]{2,1,0:T(8,128)S(1)}, f32[1,8,128]{2,1,0:T(8,128)S(1)}, u32[]{:S(2)}, u32[]{:S(2)}) collective-permute-start(f32[1,8,128]{2,1,0:T(8,128)S(1)} %get-tuple-element.12), channel_id=1, source_target_pairs={{0,4},{1,5},{2,6},{3,7},{4,0},{5,1},{6,2},{7,3},{8,12},{9,13},{10,... | collective-permute-start | bytes 12296 | tf_op jit(solution)/shard_map/ppermute | solution.py:197
  58.2 1.9 %collective-permute-done.5 = f32[1,8,128]{2,1,0:T(8,128)S(1)} collective-permute-done((f32[1,8,128]{2,1,0:T(8,128)S(1)}, f32[1,8,128]{2,1,0:T(8,128)S(1)}, u32[]{:S(2)}, u32[]{:S(2)}) %collective-permute-start.5) | collective-permute-done | bytes 4128 | tf_op jit(solution)/shard_map/ppermute | solution.py:197
  60.2 2.1 %collective-permute-start.6 = (f32[2,8,128]{2,1,0:T(8,128)S(1)}, f32[2,8,128]{2,1,0:T(8,128)S(1)}, u32[]{:S(2)}, u32[]{:S(2)}) collective-permute-start(f32[2,8,128]{2,1,0:T(8,128)S(1)} %pad_maximum_fusion.3), channel_id=1, source_target_pairs={{0,2},{1,3},{2,0},{3,1},{4,6},{5,7},{6,4},{7,5},{8,10},{9,11},{10,... | collective-permute-start | bytes 24584 | tf_op jit(solution)/shard_map/ppermute | solution.py:197
  62.3 0.7 constant_dynamic-update-slice_fusion.9
  63.0 2.3 %collective-permute-done.6 = f32[2,8,128]{2,1,0:T(8,128)S(1)} collective-permute-done((f32[2,8,128]{2,1,0:T(8,128)S(1)}, f32[2,8,128]{2,1,0:T(8,128)S(1)}, u32[]{:S(2)}, u32[]{:S(2)}) %collective-permute-start.6) | collective-permute-done | bytes 8224 | tf_op jit(solution)/shard_map/ppermute | solution.py:197
  65.3 0.5 collective-permute-start.7
  65.9 0.5 iota_xor_fusion.wanted_ref
  66.4 3.8 %all-to-all-done.1 = f32[8,48,256]{2,1,0:T(8,128)S(1)} async-done(((f32[8,48,256]{2,1,0:T(8,128)}), f32[8,48,256]{2,1,0:T(8,128)S(1)}, u32[]{:S(2)}, u32[]{:S(2)}) %all-to-all-start.1) | async-done | bytes 393248 | tf_op jit(solution)/shard_map/all_to_all | solution.py:184
  70.2 1.7 collective-permute-start.3
  71.9 0.0 collective-permute-done.7
  71.9 2.5 %collective-permute-done.3 = f32[48,256]{1,0:T(8,128)S(1)} collective-permute-done((f32[48,256]{1,0:T(8,128)S(1)}, f32[48,256]{1,0:T(8,128)S(1)}, u32[]{:S(2)}, u32[]{:S(2)}) %collective-permute-start.3) | collective-permute-done | bytes 49184 | tf_op jit(solution)/shard_map/ppermute | solution.py:183
  74.4 0.8 broadcast_in_dim.9
  75.2 3.5 %all-to-all-start.2 = ((f32[8,48,256]{2,1,0:T(8,128)}), f32[8,48,256]{2,1,0:T(8,128)S(1)}, u32[]{:S(2)}, u32[]{:S(2)}) async-start(f32[8,48,256]{2,1,0:T(8,128)} %broadcast_in_dim.9), calls=%async_computation.2 | async-start | bytes 786432 | tf_op jit(solution)/shard_map/all_to_all | solution.py:184
  78.7 13.9 %all-to-all-done.2.keep_ref = f32[8,48,256]{2,1,0:T(8,128)S(1)} async-done(((f32[8,48,256]{2,1,0:T(8,128)}), f32[8,48,256]{2,1,0:T(8,128)S(1)}, u32[]{:S(2)}, u32[]{:S(2)}) %all-to-all-start.2) | async-done | bytes 393248 | tf_op jit(solution)/shard_map/all_to_all | solution.py:184
  92.5 0.0 copy-start
  92.6 0.0 collective-permute-start.4
  92.6 0.0 copy-start.5
  92.6 0.6 copy-done.5
  93.2 4.6 %sort_rows.1.rows_ref = f32[8,8,128]{2,1,0:T(8,128)} custom-call(s32[8]{0:T(128)} %iota_xor_fusion.wanted_ref, f32[8,8,128]{2,1,0:T(8,128)} %copy-done.5), custom_call_target="tpu_custom_call" | custom-call | tf_op jit(solution)/shard_map/sort_rows/pallas_call | solution.py:244
  97.8 9.6 %gram.1.gram_ref = bf16[8,512,1024]{2,1,0:T(8,128)(2,1)} custom-call(f32[8,8,512]{2,1,0:T(8,128)} %copy-done.4, f32[8,8,128]{2,1,0:T(8,128)} %sort_rows.1.rows_ref), custom_call_target="tpu_custom_call" | custom-call | flops 83886080 | bytes 8388608 | tf_op jit(solution)/shard_map/gram/pallas_call | solution.py:136
  107.4 0.0 collective-permute-done.4.send_ref
  107.4 0.0 copy-done
  107.4 0.0 copy-start.2
  107.4 0.8 copy-done.2
  108.2 5.8 %mix.2 = f32[8,48,128]{2,1,0:T(8,128)} custom-call(f32[8,48,256]{2,1,0:T(8,128)} %copy-done, f32[8,48,256]{2,1,0:T(8,128)} %copy-done.2, bf16[8,512,1024]{2,1,0:T(8,128)(2,1)} %gram.1.gram_ref), custom_call_target="tpu_custom_call" | custom-call | flops 805306368 | bytes 10485760 | tf_op jit(solution)/shard_map/mix/pallas_call | solution.py:170
  114.0 15.0 %all_to_all.30 = f32[8,48,128]{2,1,0:T(8,128)S(1)} all-to-all(f32[8,48,128]{2,1,0:T(8,128)} %mix.2), channel_id=1, replica_groups=mesh['wide'=32,'narrow'=8] {'narrow'}, dimensions={0} | all-to-all | bytes 393216 | tf_op jit(solution)/shard_map/all_to_all | solution.py:225
  129.0 0.6 slice_add_fusion
  129.6 0.7 collective-permute-start.8
  130.3 3.1 %collective-permute-done.8 = f32[48,128]{1,0:T(8,128)S(1)} collective-permute-done((f32[48,128]{1,0:T(8,128)S(1)}, f32[48,128]{1,0:T(8,128)S(1)}, u32[]{:S(2)}, u32[]{:S(2)}) %collective-permute-start.8) | collective-permute-done | bytes 24608 | tf_op jit(solution)/shard_map/ppermute | solution.py:183
  133.5 15.4 %all_to_all.31.keep_ref = f32[8,48,256]{2,1,0:T(8,128)S(1)} all-to-all(f32[8,48,256]{2,1,0:T(8,128)S(1)} %broadcast_in_dim.11), channel_id=1, replica_groups={{0,32,64,96,128,160,192,224},{8,40,72,104,136,168,200,232},{16,48,80,11..., dimensions={0} | all-to-all | bytes 786432 | tf_op jit(solution)/shard_map/all_to_all | solution.py:184
  148.9 0.0 copy-start.1
  148.9 0.0 collective-permute-start.9
  148.9 1.7 %collective-permute-done.9.send_ref = f32[8,48,256]{2,1,0:T(8,128)S(1)} collective-permute-done((f32[8,48,256]{2,1,0:T(8,128)S(1)}, f32[8,48,256]{2,1,0:T(8,128)S(1)}, u32[]{:S(2)}, u32[]{:S(2)}) %collective-permute-start.9) | collective-permute-done | bytes 393248 | tf_op jit(solution)/shard_map/ppermute | solution.py:183
  150.6 0.0 copy-done.1
  150.6 0.0 copy-start.3
  150.6 0.8 copy-done.3
  151.4 5.8 %mix.3 = f32[8,48,128]{2,1,0:T(8,128)} custom-call(f32[8,48,256]{2,1,0:T(8,128)} %copy-done.1, f32[8,48,256]{2,1,0:T(8,128)} %copy-done.3, bf16[8,512,1024]{2,1,0:T(8,128)(2,1)} %gram.1.gram_ref), custom_call_target="tpu_custom_call" | custom-call | flops 805306368 | bytes 10485760 | tf_op jit(solution)/shard_map/mix/pallas_call | solution.py:170
  157.2 11.9 %all_to_all.32 = f32[8,48,128]{2,1,0:T(8,128)S(1)} all-to-all(f32[8,48,128]{2,1,0:T(8,128)} %mix.3), channel_id=1, replica_groups=mesh['wide'=32,'narrow'=8] {'narrow'}, dimensions={0} | all-to-all | bytes 393216 | tf_op jit(solution)/shard_map/all_to_all | solution.py:225
  169.2 0.6 add_subtract_fusion
  (19 shorter events, 0.1 us)
Async XLA Ops:
  1.3 3.6 %collective-permute-start = (f32[8,128]{1,0:T(8,128)S(1)}, f32[8,128]{1,0:T(8,128)S(1)}, u32[]{:S(2)}, u32[]{:S(2)}) collective-permute-start(f32[8,128]{1,0:T(8,128)S(1)} %get-tuple-element.13), channel_id=1, source_target_pairs={{0,16},{8,24},{16,0},{24,8},{32,48},{40,56},{48,32},{56,40},{64,80... | collective-permute-start | bytes 12296 | tf_op jit(solution)/shard_map/ppermute | solution.py:183
  5.6 16.8 %all-to-all-start = ((f32[8,8,256]{2,1,0:T(8,128)}), f32[8,8,256]{2,1,0:T(8,128)S(1)}, u32[]{:S(2)}, u32[]{:S(2)}) async-start(f32[8,8,256]{2,1,0:T(8,128)} %broadcast_in_dim.8), calls=%async_computation | async-start | bytes 131072 | tf_op jit(solution)/shard_map/all_to_all | solution.py:184
  22.4 1.3 collective-permute-start.1
  23.7 0.7 copy-start.4
  47.8 1.9 %collective-permute-start.2 = (f32[8,48,256]{2,1,0:T(8,128)}, f32[8,48,256]{2,1,0:T(8,128)S(1)}, u32[]{:S(2)}, u32[]{:S(2)}) collective-permute-start(f32[8,48,256]{2,1,0:T(8,128)} %get-tuple-element.5), channel_id=1, source_target_pairs={{0,8},{8,0},{16,24},{24,16},{32,40},{40,32},{48,56},{56,48},{64,72... | collective-permute-start | bytes 1179656 | tf_op jit(solution)/shard_map/ppermute | solution.py:183
  51.5 18.6 %all-to-all-start.1 = ((f32[8,48,256]{2,1,0:T(8,128)}), f32[8,48,256]{2,1,0:T(8,128)S(1)}, u32[]{:S(2)}, u32[]{:S(2)}) async-start(f32[8,48,256]{2,1,0:T(8,128)} %add.31), calls=%async_computation.1 | async-start | bytes 786432 | tf_op jit(solution)/shard_map/all_to_all | solution.py:184
  55.0 5.2 %collective-permute-start.5 = (f32[1,8,128]{2,1,0:T(8,128)S(1)}, f32[1,8,128]{2,1,0:T(8,128)S(1)}, u32[]{:S(2)}, u32[]{:S(2)}) collective-permute-start(f32[1,8,128]{2,1,0:T(8,128)S(1)} %get-tuple-element.12), channel_id=1, source_target_pairs={{0,4},{1,5},{2,6},{3,7},{4,0},{5,1},{6,2},{7,3},{8,12},{9,13},{10,... | collective-permute-start | bytes 12296 | tf_op jit(solution)/shard_map/ppermute | solution.py:197
  60.2 5.2 %collective-permute-start.6 = (f32[2,8,128]{2,1,0:T(8,128)S(1)}, f32[2,8,128]{2,1,0:T(8,128)S(1)}, u32[]{:S(2)}, u32[]{:S(2)}) collective-permute-start(f32[2,8,128]{2,1,0:T(8,128)S(1)} %pad_maximum_fusion.3), channel_id=1, source_target_pairs={{0,2},{1,3},{2,0},{3,1},{4,6},{5,7},{6,4},{7,5},{8,10},{9,11},{10,... | collective-permute-start | bytes 24584 | tf_op jit(solution)/shard_map/ppermute | solution.py:197
  65.3 6.5 %collective-permute-start.7 = (f32[4,8,128]{2,1,0:T(8,128)S(1)}, f32[4,8,128]{2,1,0:T(8,128)S(1)}, u32[]{:S(2)}, u32[]{:S(2)}) collective-permute-start(f32[4,8,128]{2,1,0:T(8,128)S(1)} %pad_maximum_fusion.1), channel_id=1, source_target_pairs={{0,1},{1,0},{2,3},{3,2},{4,5},{5,4},{6,7},{7,6},{8,9},{9,8},{10,11... | collective-permute-start | bytes 49160 | tf_op jit(solution)/shard_map/ppermute | solution.py:197
  70.2 4.2 %collective-permute-start.3 = (f32[48,256]{1,0:T(8,128)S(1)}, f32[48,256]{1,0:T(8,128)S(1)}, u32[]{:S(2)}, u32[]{:S(2)}) collective-permute-start(f32[48,256]{1,0:T(8,128)S(1)} %reduce_sum.27), channel_id=1, source_target_pairs={{0,16},{8,24},{16,0},{24,8},{32,48},{40,56},{48,32},{56,40},{64,80... | collective-permute-start | bytes 147464 | tf_op jit(solution)/shard_map/ppermute | solution.py:183
  75.2 17.4 %all-to-all-start.2 = ((f32[8,48,256]{2,1,0:T(8,128)}), f32[8,48,256]{2,1,0:T(8,128)S(1)}, u32[]{:S(2)}, u32[]{:S(2)}) async-start(f32[8,48,256]{2,1,0:T(8,128)} %broadcast_in_dim.9), calls=%async_computation.2 | async-start | bytes 786432 | tf_op jit(solution)/shard_map/all_to_all | solution.py:184
  92.5 14.9 %copy-start = (f32[8,48,256]{2,1,0:T(8,128)}, f32[8,48,256]{2,1,0:T(8,128)S(1)}, u32[]{:S(2)}) copy-start(f32[8,48,256]{2,1,0:T(8,128)S(1)} %all-to-all-done.2.keep_ref) | copy-start | bytes 1179652
  92.6 14.9 %collective-permute-start.4 = (f32[8,48,256]{2,1,0:T(8,128)S(1)}, f32[8,48,256]{2,1,0:T(8,128)S(1)}, u32[]{:S(2)}, u32[]{:S(2)}) collective-permute-start(f32[8,48,256]{2,1,0:T(8,128)S(1)} %all-to-all-done.2.keep_ref), channel_id=1, source_target_pairs={{0,8},{8,0},{16,24},{24,16},{32,40},{40,32},{48,56},{56,48},{64,72... | collective-permute-start | bytes 1179656 | tf_op jit(solution)/shard_map/ppermute | solution.py:183
  92.6 0.7 copy-start.5
  107.4 0.8 copy-start.2
  129.6 3.8 %collective-permute-start.8 = (f32[48,128]{1,0:T(8,128)S(1)}, f32[48,128]{1,0:T(8,128)S(1)}, u32[]{:S(2)}, u32[]{:S(2)}) collective-permute-start(f32[48,128]{1,0:T(8,128)S(1)} %get-tuple-element.7), channel_id=1, source_target_pairs={{0,16},{8,24},{16,0},{24,8},{32,48},{40,56},{48,32},{56,40},{64,80... | collective-permute-start | bytes 73736 | tf_op jit(solution)/shard_map/ppermute | solution.py:183
  148.9 1.7 %copy-start.1 = (f32[8,48,256]{2,1,0:T(8,128)}, f32[8,48,256]{2,1,0:T(8,128)S(1)}, u32[]{:S(2)}) copy-start(f32[8,48,256]{2,1,0:T(8,128)S(1)} %all_to_all.31.keep_ref) | copy-start | bytes 1179652
  148.9 1.7 %collective-permute-start.9 = (f32[8,48,256]{2,1,0:T(8,128)S(1)}, f32[8,48,256]{2,1,0:T(8,128)S(1)}, u32[]{:S(2)}, u32[]{:S(2)}) collective-permute-start(f32[8,48,256]{2,1,0:T(8,128)S(1)} %all_to_all.31.keep_ref), channel_id=1, source_target_pairs={{0,8},{8,0},{16,24},{24,16},{32,40},{40,32},{48,56},{56,48},{64,72... | collective-permute-start | bytes 1179656 | tf_op jit(solution)/shard_map/ppermute | solution.py:183
  150.6 0.8 copy-start.3

commit v2 on v0

v2 whole, which is shorter than its diff:
```python
import functools
import math

import jax
import jax.numpy as jnp
from jax import lax
from jax.experimental import pallas as pl
from jax.experimental.pallas import tpu as pltpu
from jax.sharding import PartitionSpec as P


TILE = 128
RADIUS = 0.15
KERNEL_GAIN = 3200.0
RHS_GAIN = 28.0
LOWER_EDGE = 1.0
UPPER_EDGE = 4.0

SCALE = 4.0 / RADIUS
PHI = 1.0 / 256.0
FAR = 4096.0
DEPTH = 128
GRANT = 20 << 20


def split3(x):
    one = x.astype(jnp.bfloat16).astype(jnp.float32)
    rest = x - one
    two = rest.astype(jnp.bfloat16).astype(jnp.float32)
    return one, two, rest - two


def padded(points):
    fill = jnp.full((8 - points.shape[0], points.shape[1]), 0.5, jnp.float32)
    return jnp.concatenate([points, fill], axis=0)


def features(points, target, extra=None):
    count = points.shape[1]
    centred = (points - 0.5) * SCALE
    norm = jnp.sum(centred * centred, axis=0, keepdims=True)
    n1, n2, n3 = split3(jnp.broadcast_to(norm, (8, count)))
    row = lax.broadcasted_iota(jnp.int32, (8, count), 0)
    one, zero = jnp.ones_like(n1), jnp.zeros_like(n1)
    if target:
        c1, c2, c3 = split3(-2.0 * centred)
        tail = jnp.where(row < 3, one, jnp.where(row == 3, n1, jnp.where(row == 4, n2, jnp.where(row == 5, n3, zero))))
        groups = [c1, c2, c1, c2, c3, c1, tail]
    else:
        c1, c2, c3 = split3(centred)
        tail = jnp.where(row == 0, n1, jnp.where(row == 1, n2, jnp.where(row == 2, n3, jnp.where(row < 6, one, zero))))
        groups = [c1, c1, c2, c2, c1, c3, tail]
    used = 8 * len(groups)
    if extra is not None:
        groups.append(extra)
        used += extra.shape[0]
    groups.append(jnp.zeros((DEPTH - used, count), jnp.float32))
    return jnp.concatenate(groups, axis=0)


def profile(d2):
    d2 = jnp.maximum(d2, 1e-12)
    w = jnp.maximum(4.0 - d2 * lax.rsqrt(d2), 0.0)
    square = w * w
    return (square * square) * (5.0 - w)


def stage_kernel(vol_ref, adj_ref, mask_ref, feat_ref, weights_ref, absent_ref, near_ref, held_ref, sem_ref):
    copies = [
        pltpu.make_async_copy(vol_ref, near_ref, sem_ref.at[0]),
        pltpu.make_async_copy(mask_ref, held_ref, sem_ref.at[1]),
        pltpu.make_async_copy(adj_ref, weights_ref, sem_ref.at[2]),
    ]
    for copy in copies:
        copy.start()
    for copy in copies:
        copy.wait()
    rows = vol_ref.shape[1]
    tiles = rows // TILE
    tile = lax.broadcasted_iota(jnp.int32, (tiles, rows), 0)
    place = lax.broadcasted_iota(jnp.int32, (tiles, rows), 1) // TILE
    onehot = jnp.where(tile == place, 1.0, 0.0)
    feat_ref[...] = features(padded(near_ref[...]), False, onehot).T.astype(jnp.bfloat16)
    absent_ref[...] = (1 - held_ref[...]).astype(jnp.float32)


def stage(vol, adj, mask):
    return pl.pallas_call(
        stage_kernel,
        in_specs=[pl.BlockSpec(memory_space=pltpu.HBM)] * 3,
        out_specs=[pl.BlockSpec(memory_space=pltpu.VMEM)] * 3,
        out_shape=(
            jax.ShapeDtypeStruct((vol.shape[1], DEPTH), jnp.bfloat16),
            jax.ShapeDtypeStruct(adj.shape, jnp.bfloat16),
            jax.ShapeDtypeStruct(mask.shape, jnp.float32),
        ),
        scratch_shapes=[
            pltpu.VMEM(vol.shape, jnp.float32),
            pltpu.VMEM(mask.shape, jnp.int32),
            pltpu.SemaphoreType.DMA((3,)),
        ],
        name="stage",
        compiler_params=pltpu.CompilerParams(vmem_limit_bytes=GRANT),
        cost_estimate=pl.CostEstimate(flops=1 << 20, bytes_accessed=2 << 20, transcendentals=0),
    )(*[pltpu.with_memory_space_constraint(x, pltpu.HBM) for x in (vol, adj, mask)])


def coupling_kernel(base, spot_ref, feat_ref, adj_ref, absent_ref, cols_ref, *refs):
    keep_ref, send_ref = refs[-2:]
    rows = feat_ref.shape[0]
    width = cols_ref.shape[2]
    far = (base + pl.program_id(0)) ^ spot_ref[1]

    cols_tiles = absent_ref.shape[1]
    tile = lax.broadcasted_iota(jnp.int32, (cols_tiles, width), 0)
    piece = lax.broadcasted_iota(jnp.int32, (cols_tiles, width), 1) // TILE
    swapped = (piece % 2) * 2 + piece // 2
    pick = jnp.where(tile == 4 * far + (swapped ^ spot_ref[0]), 1.0, 0.0).astype(jnp.bfloat16)
    barred = FAR * jnp.dot(absent_ref[...].astype(jnp.bfloat16), pick, preferred_element_type=jnp.float32)
    target = features(cols_ref[0], True, barred).astype(jnp.bfloat16)

    half = width // 2
    step = 512
    lower = (spot_ref[0] >> 1) & 1
    for side, out_ref in enumerate((keep_ref, send_ref)):
        total = jnp.zeros((adj_ref.shape[0], half), jnp.float32)
        for start in range(0, rows, step):
            d2 = jnp.dot(
                feat_ref[start:start + step, :],
                target[:, side * half:(side + 1) * half],
                preferred_element_type=jnp.float32,
            )
            values = profile(d2).astype(jnp.bfloat16)
            total += jnp.dot(adj_ref[:, start:start + step], values, preferred_element_type=jnp.float32)
        out_ref[lower] = total[:, :TILE]
        out_ref[1 - lower] = total[:, TILE:]


def coupling(base, blocks, spot, staged, cols, earlier=None):
    feat, adj, absent = staged
    count, _, width = cols.shape
    objs = adj.shape[0]
    whole = lambda shape: pl.BlockSpec(shape, lambda i, s: (0,) * len(shape))
    out = jax.ShapeDtypeStruct((2 * blocks, objs, TILE), jnp.float32)
    place = pl.BlockSpec((2, objs, TILE), lambda i, s: ((base + i) ^ s[1], 0, 0))
    extra = () if earlier is None else tuple(earlier)
    return pl.pallas_call(
        functools.partial(coupling_kernel, base),
        grid_spec=pltpu.PrefetchScalarGridSpec(
            num_scalar_prefetch=1,
            grid=(count,),
            in_specs=[
                whole(feat.shape),
                whole(adj.shape),
                whole(absent.shape),
                pl.BlockSpec((1, 8, width), lambda i, s: (i, 0, 0)),
            ] + [pl.BlockSpec(memory_space=pl.ANY)] * len(extra),
            out_specs=[place] * 2,
        ),
        out_shape=(out, out),
        input_output_aliases={5 + i: i for i in range(len(extra))},
        compiler_params=pltpu.CompilerParams(vmem_limit_bytes=GRANT),
        cost_estimate=pl.CostEstimate(flops=20 * feat.shape[0] * count * width, bytes_accessed=2 << 20, transcendentals=0),
    )(spot, feat, adj, absent, cols, *extra)


def gram_kernel(spot_ref, near_ref, far_ref, rows_ref, out_ref, feat_ref):
    @pl.when(pl.program_id(0) == 0)
    def _():
        for j in range(rows_ref.shape[0]):
            feat_ref[:, j * TILE:(j + 1) * TILE] = features(rows_ref[j ^ spot_ref[2]], True).astype(jnp.bfloat16)

    held = near_ref.shape[0]
    block = pl.program_id(0) ^ spot_ref[1]
    slot = lax.rem(block, held)
    points = jnp.where(block < held, near_ref[slot], far_ref[slot])
    lower = (spot_ref[0] >> 1) & 1
    width = out_ref.shape[3]
    step = 256
    for side in range(2):
        one = points[:, 2 * side * TILE:(2 * side + 1) * TILE]
        two = points[:, (2 * side + 1) * TILE:(2 * side + 2) * TILE]
        pair = jnp.where(lower == 0, jnp.concatenate([one, two], axis=1), jnp.concatenate([two, one], axis=1))
        source = features(pair, False).T.astype(jnp.bfloat16)
        for start in range(0, width, step):
            d2 = jnp.dot(source, feat_ref[:, start:start + step], preferred_element_type=jnp.float32)
            out_ref[side, 0, :, start:start + step] = profile(d2).astype(jnp.bfloat16)


def gram(spot, near, far, rows):
    blocks = 2 * near.shape[0]
    width = rows.shape[0] * rows.shape[2]
    whole = lambda shape: pl.BlockSpec(shape, lambda z, s: (0,) * len(shape))
    return pl.pallas_call(
        gram_kernel,
        grid_spec=pltpu.PrefetchScalarGridSpec(
            num_scalar_prefetch=1,
            grid=(blocks,),
            in_specs=[whole(near.shape), whole(far.shape), whole(rows.shape)],
            out_specs=pl.BlockSpec((2, 1, 2 * TILE, width), lambda z, s: (0, z, 0, 0)),
            scratch_shapes=[pltpu.VMEM((DEPTH, width), jnp.bfloat16)],
        ),
        out_shape=pltpu.HBM((2, blocks, 2 * TILE, width), jnp.bfloat16),
        name="gram",
        compiler_params=pltpu.CompilerParams(vmem_limit_bytes=GRANT),
        cost_estimate=pl.CostEstimate(flops=40 * blocks * TILE * width, bytes_accessed=8 << 20, transcendentals=0),
    )(spot, near, far, rows)


def mix_kernel(side, field_ref, gram_ref, *refs):
    out_ref, held_ref, sem_ref = refs[-3:]
    blocks, _, width = held_ref.shape
    objs = field_ref.shape[1]
    copies = [pltpu.make_async_copy(gram_ref.at[side, z], held_ref.at[z], sem_ref.at[z]) for z in range(blocks)]
    for copy in copies:
        copy.start()
    total = jnp.zeros((2 * objs, width), jnp.float32)
    for z in range(blocks):
        field = jnp.concatenate([field_ref[2 * z], field_ref[2 * z + 1]], axis=1)
        high = field.astype(jnp.bfloat16).astype(jnp.float32)
        both = jnp.concatenate([high, field - high], axis=0).astype(jnp.bfloat16)
        copies[z].wait()
        total += jnp.dot(both, held_ref[z], preferred_element_type=jnp.float32)
    for j in range(out_ref.shape[0]):
        part = total[:objs, j * TILE:(j + 1) * TILE] + total[objs:, j * TILE:(j + 1) * TILE]
        out_ref[j] = part if side == 0 else part + refs[0][j]


def mix(side, field, block, earlier=()):
    _, objs, _ = field.shape
    _, blocks, depth, width = block.shape
    parts = width // TILE
    return pl.pallas_call(
        functools.partial(mix_kernel, side),
        in_specs=[pl.BlockSpec(memory_space=pltpu.VMEM), pl.BlockSpec(memory_space=pltpu.HBM)]
        + [pl.BlockSpec(memory_space=pltpu.VMEM)] * len(earlier),
        out_specs=pl.BlockSpec(memory_space=pltpu.VMEM),
        out_shape=jax.ShapeDtypeStruct((parts, objs, TILE), jnp.float32),
        scratch_shapes=[pltpu.VMEM((blocks, depth, width), jnp.bfloat16), pltpu.SemaphoreType.DMA((blocks,))],
        name="mix",
        compiler_params=pltpu.CompilerParams(vmem_limit_bytes=GRANT),
        cost_estimate=pl.CostEstimate(flops=4 * objs * blocks * depth * width, bytes_accessed=5 << 20, transcendentals=0),
    )(field, pltpu.with_memory_space_constraint(block, pltpu.HBM), *earlier)


def body(n_wide, n_narrow, vol_points, vol_adjoint, surf_points, tile_mask):
    half = n_wide // 2
    groups = [[2 * k + core for k in range(half)] for core in range(2)]
    swap = lambda x, bit: lax.ppermute(x, "wide", [(i, i ^ bit) for i in range(n_wide)])
    side = lambda x, bit: lax.ppermute(x, "narrow", [(i, i ^ bit) for i in range(n_narrow)])
    flip = lambda x: swap(x, 1)
    exchange = lambda x: lax.all_to_all(x, "wide", 0, 0, axis_index_groups=groups, tiled=True)
    repeat = lambda x, count: jnp.broadcast_to(x[None], (count,) + x.shape)
    join = lambda x, y: jnp.concatenate([x, y], axis=0)

    wide = lax.axis_index("wide").astype(jnp.int32)
    spot = jnp.stack([wide & 3, wide >> 2, lax.axis_index("narrow").astype(jnp.int32)])
    own = jnp.pad(surf_points, ((0, 5), (0, 0)), constant_values=0.5)
    far = n_wide // 4
    staged = stage(vol_points, vol_adjoint, tile_mask)
    pair = jnp.concatenate([own, swap(own, 2)], axis=1)
    rows = join(own[None], side(own[None], 1))
    quad = jnp.concatenate([pair, flip(pair)], axis=1)[None]
    rows = join(rows, side(rows, 2))
    two = join(quad, swap(quad, 4))
    rows = join(rows, side(rows, 4))
    next_two = swap(two, 8)
    sums = coupling(0, far, spot, staged, two)
    four = join(two, next_two)
    next_four = swap(four, 16)
    sums = coupling(2, far, spot, staged, next_two, sums)
    keep, send = coupling(4, far, spot, staged, next_four, sums)
    got = flip(send)
    block = gram(spot, four, next_four, rows)
    parts = exchange(keep + got)

    total_volume = vol_points.shape[1] * n_wide
    total_surface = surf_points.shape[1] * n_wide * n_narrow
    centre = (LOWER_EDGE + UPPER_EDGE) / 2.0
    half_width = (UPPER_EDGE - LOWER_EDGE) / 2.0
    sigma = centre / half_width
    rho_zero = 1.0 / sigma
    rho_one = 1.0 / (2.0 * sigma - rho_zero)
    gain = KERNEL_GAIN / total_surface * PHI

    def mixed(field):
        mine = exchange(repeat(field, half))
        other = flip(mine)
        partial = mix(0, mine, block)
        partial = mix(1, other, block, (partial,))
        return add_up(lax.all_to_all(partial, "narrow", 0, 0, tiled=True))

    rhs = add_up(parts) * (RHS_GAIN / math.sqrt(total_volume) * PHI)
    first = rhs / centre
    near = rhs - (first + gain * mixed(first))
    update = rho_one * rho_zero * first + 2.0 * rho_one / half_width * near
    solution = first + update
    residual = near - (update + gain * mixed(update))
    return (solution, residual)


def add_up(parts):
    total = parts[0]
    for k in range(1, parts.shape[0]):
        total = total + parts[k]
    return total


def solution(mesh):
    return jax.shard_map(
        functools.partial(body, mesh.shape["wide"], mesh.shape["narrow"]),
        mesh=mesh,
        in_specs=(
            P(None, "wide"),
            P(None, "wide"),
            P(None, ("narrow", "wide")),
            P("wide", "narrow"),
        ),
        out_specs=(P(None, ("narrow", "wide")), P(None, ("narrow", "wide"))),
        check_vma=False,
    )
```

time: 495 us -> 150 us (0.30)
  waiting for transfers between devices: 227 us -> 26.1 us
  matrix products: 81.2 us -> 0 us
  blocking collectives: 136 us -> 59.4 us
  Pallas kernels: 0 us -> 37.4 us
  starting transfers between devices: 0.12 us -> 22.9 us
  other arithmetic: 16.1 us -> 0.83 us
  local copies, waits for them, and re-layouts: 16.7 us -> 1.49 us
  between operations: 13.8 us -> 0.75 us
    reduce_scatter x3 -> x0, waiting for transfers between devices: 227 us -> none  [the longest x2 142 us: apply_operator(): lax.psum_scatter(partial_rows, 'narrow', scatter_dimension=1, tiled=True)]
    all_gather x4 -> x0, blocking collectives: 136 us -> none  [the longest x2 68.4 us: apply_operator(): piece = lax.all_gather(field, 'wide', axis=1, tiled=True)]
    dot_general x48 -> x0, matrix products: 81.2 us -> none  [the longest x32 51.3 us: one_block(): jnp.dot(block_vals, values, precision=lax.Precision.HIGHEST, preferred_el...]
    all_to_all x0 -> x4, blocking collectives: none -> 59.4 us  [the longest x2 33.7 us: body(): lax.all_to_all(x, 'wide', 0, 0, axis_index_groups=groups, tiled=True)]
    pallas_call x0 -> x9, Pallas kernels: none -> 37.4 us  [the longest x3 16.6 us: coupling(): pl.pallas_call(functools.partial(coupling_kernel, base), grid_spec=pltpu....]
    ppermute x0 -> x11, starting transfers between devices: none -> 19.4 us  [the longest x8 13.6 us: body(): lax.ppermute(x, 'wide', [(i, i ^ bit) for i in range(n_wide)])]
    all_to_all x0 -> x1, waiting for transfers between devices: none -> 13.4 us  [body(): lax.all_to_all(x, 'wide', 0, 0, axis_index_groups=groups, tiled=True)]
    convert_element_type x16 -> x0, other arithmetic: 13.2 us -> none  [surface_block(): expanded = expanded.reshape(volume_rows, width).astype(jnp.float32)]
  transfers between devices with their start and end apart: 3 -> 12, of which waited for: 3 -> 8; matrix products, arithmetic and copies ran while one was open for 0% -> 0% of each run, Pallas kernels for 0% -> 16%
where the time goes in v2:
time: 150 us; the launch traced here: 149 us
  blocking collectives  59.4 us (40%)
  Pallas kernels  37.4 us (25%)
  waiting for transfers between devices  26.1 us (17%)
  starting transfers between devices  22.9 us (15%)
    all_to_all x2, blocking collectives, body(): lax.all_to_all(x, 'wide', 0, 0, axis_index_groups=groups, tiled=True)  33.7 us
    all_to_all x2, blocking collectives, mixed(): return add_up(lax.all_to_all(partial, 'narrow', 0, 0, tiled=True))  25.7 us
    pallas_call x3, Pallas kernels, coupling(): pl.pallas_call(functools.partial(coupling_kernel, base), grid_spec=pltpu....  16.6 us
    ppermute x8, starting transfers between devices, body(): lax.ppermute(x, 'wide', [(i, i ^ bit) for i in range(n_wide)])  13.6 us
    all_to_all x1, waiting for transfers between devices, body(): lax.all_to_all(x, 'wide', 0, 0, axis_index_groups=groups, tiled=True)  13.4 us
    pallas_call x4, Pallas kernels, mix(): pl.pallas_call(functools.partial(mix_kernel, side), in_specs=[pl.BlockSpe...  9.76 us
    pallas_call x1, Pallas kernels, gram(): pl.pallas_call(gram_kernel, grid_spec=pltpu.PrefetchScalarGridSpec(num_sc...  9.74 us
    ppermute x8, waiting for transfers between devices, body(): lax.ppermute(x, 'wide', [(i, i ^ bit) for i in range(n_wide)])  7.43 us
  transfers between devices with their start and end apart: 12, of which 8 were waited for; matrix products, arithmetic and copies ran while one was open for 0% of the time, Pallas kernels for 16%

profile of v2, /device:TPU:2, one launch (start us, length us, event | category | flops | bytes accessed | tf_op | source)
XLA Modules:
  0.0 148.9 jit_solution(2411854652806960777)
XLA Ops:
  0.6 0.7 pad_bitcast_fusion
  1.3 1.6 %collective-permute-start = (f32[8,128]{1,0:T(8,128)S(1)}, f32[8,128]{1,0:T(8,128)S(1)}, u32[]{:S(2)}, u32[]{:S(2)}) collective-permute-start(f32[8,128]{1,0:T(8,128)S(1)} %get-tuple-element.27), channel_id=1, source_target_pairs={{0,16},{8,24},{16,0},{24,8},{32,48},{40,56},{48,32},{56,40},{64,80... | collective-permute-start | bytes 12296 | tf_op jit(solution)/shard_map/ppermute | solution.py:249
  2.9 2.0 %collective-permute-done = f32[8,128]{1,0:T(8,128)S(1)} collective-permute-done((f32[8,128]{1,0:T(8,128)S(1)}, f32[8,128]{1,0:T(8,128)S(1)}, u32[]{:S(2)}, u32[]{:S(2)}) %collective-permute-start) | collective-permute-done | bytes 4128 | tf_op jit(solution)/shard_map/ppermute | solution.py:249
  4.9 0.0 collective-permute-start.1
  4.9 1.2 collective-permute-done.1
  6.1 1.9 %collective-permute-start.2 = (f32[1,8,512]{2,1,0:T(8,128)S(1)}, f32[1,8,512]{2,1,0:T(8,128)S(1)}, u32[]{:S(2)}, u32[]{:S(2)}) collective-permute-start(f32[1,8,512]{2,1,0:T(8,128)S(1)} %maximum_bitcast_fusion), channel_id=1, source_target_pairs={{0,32},{8,40},{16,48},{24,56},{32,0},{40,8},{48,16},{56,24},{64,96... | collective-permute-start | bytes 49160 | tf_op jit(solution)/shard_map/ppermute | solution.py:249
  8.0 1.8 %collective-permute-done.2 = f32[1,8,512]{2,1,0:T(8,128)S(1)} collective-permute-done((f32[1,8,512]{2,1,0:T(8,128)S(1)}, f32[1,8,512]{2,1,0:T(8,128)S(1)}, u32[]{:S(2)}, u32[]{:S(2)}) %collective-permute-start.2) | collective-permute-done | bytes 16416 | tf_op jit(solution)/shard_map/ppermute | solution.py:249
  9.8 3.3 %collective-permute-start.3 = (f32[2,8,512]{2,1,0:T(8,128)S(1)}, f32[2,8,512]{2,1,0:T(8,128)S(1)}, u32[]{:S(2)}, u32[]{:S(2)}) collective-permute-start(f32[2,8,512]{2,1,0:T(8,128)S(1)} %pad_maximum_fusion.1.cols_ref), channel_id=1, source_target_pairs={{0,64},{8,72},{16,80},{24,88},{32,96},{40,104},{48,112},{56,120},{... | collective-permute-start | bytes 98312 | tf_op jit(solution)/shard_map/ppermute | solution.py:249
  13.1 1.2 stage.1
  14.4 0.7 collective-permute-done.3.cols_ref
  15.0 6.8 %collective-permute-start.4 = (f32[4,8,512]{2,1,0:T(8,128)S(1)}, f32[4,8,512]{2,1,0:T(8,128)S(1)}, u32[]{:S(2)}, u32[]{:S(2)}) collective-permute-start(f32[4,8,512]{2,1,0:T(8,128)S(1)} %pad_maximum_fusion.near_ref), channel_id=1, source_target_pairs={{0,128},{8,136},{16,144},{24,152},{32,160},{40,168},{48,176},{56,1... | collective-permute-start | bytes 196616 | tf_op jit(solution)/shard_map/ppermute | solution.py:249
  21.9 0.1 pad_add_fusion.spot_ref
  22.0 4.3 %shard_map.59 = (f32[16,48,128]{2,1,0:T(8,128)S(1)}, f32[16,48,128]{2,1,0:T(8,128)S(1)}) custom-call(s32[3]{0:T(128)S(1)} %pad_add_fusion.spot_ref, bf16[2048,128]{1,0:T(8,128)(2,1)S(1)} %get-tuple-element.11.feat_ref, bf16[48,2048]{1,0:T(8,128)(2,1)S(1)} %get-tuple-element.12.adj_ref, f32[16,32]{1,0:T(8,128)S(1)} %get-tuple-element.13.absent_ref, ...), custom_call_target="tpu_custom_call" | custom-call | flops 41943040 | bytes 2097152 | tf_op jit(solution)/shard_map/pallas_call | solution.py:147
  26.2 4.3 %shard_map.60 = (f32[16,48,128]{2,1,0:T(8,128)S(1)}, f32[16,48,128]{2,1,0:T(8,128)S(1)}) custom-call(s32[3]{0:T(128)S(1)} %pad_add_fusion.spot_ref, bf16[2048,128]{1,0:T(8,128)(2,1)S(1)} %get-tuple-element.11.feat_ref, bf16[48,2048]{1,0:T(8,128)(2,1)S(1)} %get-tuple-element.12.adj_ref, ...), custom_call_target="tpu_custom_call", output_to_operand_aliasing={{0}: (5, {}), {1}: (6, {})} | custom-call | flops 41943040 | bytes 2097152 | tf_op jit(solution)/shard_map/pallas_call | solution.py:147
  30.5 0.0 collective-permute-done.4.cols_ref.far_ref
  30.6 8.0 %shard_map.61 = (f32[16,48,128]{2,1,0:T(8,128)S(1)}, f32[16,48,128]{2,1,0:T(8,128)S(1)}) custom-call(s32[3]{0:T(128)S(1)} %pad_add_fusion.spot_ref, bf16[2048,128]{1,0:T(8,128)(2,1)S(1)} %get-tuple-element.11.feat_ref, bf16[48,2048]{1,0:T(8,128)(2,1)S(1)} %get-tuple-element.12.adj_ref, ...), custom_call_target="tpu_custom_call", output_to_operand_aliasing={{0}: (5, {}), {1}: (6, {})} | custom-call | flops 83886080 | bytes 2097152 | tf_op jit(solution)/shard_map/pallas_call | solution.py:147
  38.6 0.0 collective-permute-start.5
  38.6 1.7 %collective-permute-done.5 = f32[16,48,128]{2,1,0:T(8,128)S(1)} collective-permute-done((f32[16,48,128]{2,1,0:T(8,128)S(1)}, f32[16,48,128]{2,1,0:T(8,128)S(1)}, u32[]{:S(2)}, u32[]{:S(2)}) %collective-permute-start.5) | collective-permute-done | bytes 393248 | tf_op jit(solution)/shard_map/ppermute | solution.py:249
  40.4 19.1 %all_to_all.25 = f32[16,48,128]{2,1,0:T(8,128)S(1)} all-to-all(f32[16,48,128]{2,1,0:T(8,128)S(1)} %add.193), channel_id=1, replica_groups={{0,16,32,48,64,80,96,112,128,144,160,176,192,208,224,240},{8,24,40,56,7..., dimensions={0} | all-to-all | bytes 786432 | tf_op jit(solution)/shard_map/all_to_all | solution.py:252
  59.5 0.8 broadcast_in_dim.25
  60.3 3.6 %all-to-all-start.1 = ((f32[16,48,128]{2,1,0:T(8,128)}), f32[16,48,128]{2,1,0:T(8,128)S(1)}, u32[]{:S(2)}, u32[]{:S(2)}) async-start(f32[16,48,128]{2,1,0:T(8,128)} %broadcast_in_dim.25), calls=%async_computation.1 | async-start | bytes 786432 | tf_op jit(solution)/shard_map/all_to_all | solution.py:252
  63.8 0.6 collective-permute-start.7
  64.5 13.4 %all-to-all-done.1.field_ref = f32[16,48,128]{2,1,0:T(8,128)S(1)} async-done(((f32[16,48,128]{2,1,0:T(8,128)}), f32[16,48,128]{2,1,0:T(8,128)S(1)}, u32[]{:S(2)}, u32[]{:S(2)}) %all-to-all-start.1) | async-done | bytes 393248 | tf_op jit(solution)/shard_map/all_to_all | solution.py:252
  77.8 0.0 collective-permute-start.6
  77.8 0.0 collective-permute-done.7
  77.8 2.2 %collective-permute-start.8 = (f32[2,8,128]{2,1,0:T(8,128)S(1)}, f32[2,8,128]{2,1,0:T(8,128)S(1)}, u32[]{:S(2)}, u32[]{:S(2)}) collective-permute-start(f32[2,8,128]{2,1,0:T(8,128)S(1)} %pad_maximum_fusion.5), channel_id=1, source_target_pairs={{0,2},{1,3},{2,0},{3,1},{4,6},{5,7},{6,4},{7,5},{8,10},{9,11},{10,... | collective-permute-start | bytes 24584 | tf_op jit(solution)/shard_map/ppermute | solution.py:250
  80.0 3.0 %collective-permute-done.8 = f32[2,8,128]{2,1,0:T(8,128)S(1)} collective-permute-done((f32[2,8,128]{2,1,0:T(8,128)S(1)}, f32[2,8,128]{2,1,0:T(8,128)S(1)}, u32[]{:S(2)}, u32[]{:S(2)}) %collective-permute-start.8) | collective-permute-done | bytes 8224 | tf_op jit(solution)/shard_map/ppermute | solution.py:250
  83.1 2.9 %collective-permute-start.9 = (f32[4,8,128]{2,1,0:T(8,128)S(1)}, f32[4,8,128]{2,1,0:T(8,128)S(1)}, u32[]{:S(2)}, u32[]{:S(2)}) collective-permute-start(f32[4,8,128]{2,1,0:T(8,128)S(1)} %pad_maximum_fusion.3), channel_id=1, source_target_pairs={{0,4},{1,5},{2,6},{3,7},{4,0},{5,1},{6,2},{7,3},{8,12},{9,13},{10,... | collective-permute-start | bytes 49160 | tf_op jit(solution)/shard_map/ppermute | solution.py:250
  86.0 2.3 %collective-permute-done.9 = f32[4,8,128]{2,1,0:T(8,128)S(1)} collective-permute-done((f32[4,8,128]{2,1,0:T(8,128)S(1)}, f32[4,8,128]{2,1,0:T(8,128)S(1)}, u32[]{:S(2)}, u32[]{:S(2)}) %collective-permute-start.9) | collective-permute-done | bytes 16416 | tf_op jit(solution)/shard_map/ppermute | solution.py:250
  88.3 9.7 %gram.1.gram_ref = bf16[2,8,256,1024]{3,2,1,0:T(8,128)(2,1)} custom-call(s32[3]{0:T(128)S(1)} %pad_add_fusion.spot_ref, f32[4,8,512]{2,1,0:T(8,128)S(1)} %pad_maximum_fusion.near_ref, f32[4,8,512]{2,1,0:T(8,128)S(1)} %collective-permute-done.4.cols_ref.far_ref, f32[8,8,128]{2,1,0:T(8,128)S(1)} %pad_maximum_fusion.2.rows_ref), custom_call_target="tpu_custom_call" | custom-call | flops 41943040 | bytes 8388608 | tf_op jit(solution)/shard_map/gram/pallas_call | solution.py:194
  98.1 2.4 %mix.4.refs_0_ = f32[8,48,128]{2,1,0:T(8,128)S(1)} custom-call(f32[16,48,128]{2,1,0:T(8,128)S(1)} %all-to-all-done.1.field_ref, bf16[2,8,256,1024]{3,2,1,0:T(8,128)(2,1)} %gram.1.gram_ref), custom_call_target="tpu_custom_call" | custom-call | flops 402653184 | bytes 5242880 | tf_op jit(solution)/shard_map/mix/pallas_call | solution.py:233
  100.5 0.0 collective-permute-done.6.field_ref
  100.5 2.4 %mix.5 = f32[8,48,128]{2,1,0:T(8,128)S(1)} custom-call(f32[16,48,128]{2,1,0:T(8,128)S(1)} %collective-permute-done.6.field_ref, bf16[2,8,256,1024]{3,2,1,0:T(8,128)(2,1)} %gram.1.gram_ref, f32[8,48,128]{2,1,0:T(8,128)S(1)} %mix.4.refs_0_), custom_call_target="tpu_custom_call" | custom-call | flops 402653184 | bytes 5242880 | tf_op jit(solution)/shard_map/mix/pallas_call | solution.py:233
  103.0 14.2 %all_to_all.26 = f32[8,48,128]{2,1,0:T(8,128)S(1)} all-to-all(f32[8,48,128]{2,1,0:T(8,128)S(1)} %mix.5), channel_id=1, replica_groups=mesh['wide'=32,'narrow'=8] {'narrow'}, dimensions={0} | all-to-all | bytes 393216 | tf_op jit(solution)/shard_map/all_to_all | solution.py:291
  117.3 14.7 %all_to_all.27.field_ref = f32[16,48,128]{2,1,0:T(8,128)S(1)} all-to-all(f32[16,48,128]{2,1,0:T(8,128)S(1)} %broadcast_in_dim.28), channel_id=1, replica_groups={{0,16,32,48,64,80,96,112,128,144,160,176,192,208,224,240},{8,24,40,56,7..., dimensions={0} | all-to-all | bytes 786432 | tf_op jit(solution)/shard_map/all_to_all | solution.py:252
  131.9 0.0 collective-permute-start.10
  131.9 2.4 %mix.6.refs_0_ = f32[8,48,128]{2,1,0:T(8,128)S(1)} custom-call(f32[16,48,128]{2,1,0:T(8,128)S(1)} %all_to_all.27.field_ref, bf16[2,8,256,1024]{3,2,1,0:T(8,128)(2,1)} %gram.1.gram_ref), custom_call_target="tpu_custom_call" | custom-call | flops 402653184 | bytes 5242880 | tf_op jit(solution)/shard_map/mix/pallas_call | solution.py:233
  134.4 0.0 collective-permute-done.10.field_ref
  134.4 2.4 %mix.7 = f32[8,48,128]{2,1,0:T(8,128)S(1)} custom-call(f32[16,48,128]{2,1,0:T(8,128)S(1)} %collective-permute-done.10.field_ref, bf16[2,8,256,1024]{3,2,1,0:T(8,128)(2,1)} %gram.1.gram_ref, f32[8,48,128]{2,1,0:T(8,128)S(1)} %mix.6.refs_0_), custom_call_target="tpu_custom_call" | custom-call | flops 402653184 | bytes 5242880 | tf_op jit(solution)/shard_map/mix/pallas_call | solution.py:233
  136.8 11.4 %all_to_all.28 = f32[8,48,128]{2,1,0:T(8,128)S(1)} all-to-all(f32[8,48,128]{2,1,0:T(8,128)S(1)} %mix.7), channel_id=1, replica_groups=mesh['wide'=32,'narrow'=8] {'narrow'}, dimensions={0} | all-to-all | bytes 393216 | tf_op jit(solution)/shard_map/all_to_all | solution.py:291
  148.3 0.6 fusion.3
  (11 shorter events, 0.1 us)
Async XLA Ops:
  1.3 3.6 %collective-permute-start = (f32[8,128]{1,0:T(8,128)S(1)}, f32[8,128]{1,0:T(8,128)S(1)}, u32[]{:S(2)}, u32[]{:S(2)}) collective-permute-start(f32[8,128]{1,0:T(8,128)S(1)} %get-tuple-element.27), channel_id=1, source_target_pairs={{0,16},{8,24},{16,0},{24,8},{32,48},{40,56},{48,32},{56,40},{64,80... | collective-permute-start | bytes 12296 | tf_op jit(solution)/shard_map/ppermute | solution.py:249
  4.9 1.2 collective-permute-start.1
  6.1 3.7 %collective-permute-start.2 = (f32[1,8,512]{2,1,0:T(8,128)S(1)}, f32[1,8,512]{2,1,0:T(8,128)S(1)}, u32[]{:S(2)}, u32[]{:S(2)}) collective-permute-start(f32[1,8,512]{2,1,0:T(8,128)S(1)} %maximum_bitcast_fusion), channel_id=1, source_target_pairs={{0,32},{8,40},{16,48},{24,56},{32,0},{40,8},{48,16},{56,24},{64,96... | collective-permute-start | bytes 49160 | tf_op jit(solution)/shard_map/ppermute | solution.py:249
  9.8 5.2 %collective-permute-start.3 = (f32[2,8,512]{2,1,0:T(8,128)S(1)}, f32[2,8,512]{2,1,0:T(8,128)S(1)}, u32[]{:S(2)}, u32[]{:S(2)}) collective-permute-start(f32[2,8,512]{2,1,0:T(8,128)S(1)} %pad_maximum_fusion.1.cols_ref), channel_id=1, source_target_pairs={{0,64},{8,72},{16,80},{24,88},{32,96},{40,104},{48,112},{56,120},{... | collective-permute-start | bytes 98312 | tf_op jit(solution)/shard_map/ppermute | solution.py:249
  15.0 15.5 %collective-permute-start.4 = (f32[4,8,512]{2,1,0:T(8,128)S(1)}, f32[4,8,512]{2,1,0:T(8,128)S(1)}, u32[]{:S(2)}, u32[]{:S(2)}) collective-permute-start(f32[4,8,512]{2,1,0:T(8,128)S(1)} %pad_maximum_fusion.near_ref), channel_id=1, source_target_pairs={{0,128},{8,136},{16,144},{24,152},{32,160},{40,168},{48,176},{56,1... | collective-permute-start | bytes 196616 | tf_op jit(solution)/shard_map/ppermute | solution.py:249
  38.6 1.8 %collective-permute-start.5 = (f32[16,48,128]{2,1,0:T(8,128)S(1)}, f32[16,48,128]{2,1,0:T(8,128)S(1)}, u32[]{:S(2)}, u32[]{:S(2)}) collective-permute-start(f32[16,48,128]{2,1,0:T(8,128)S(1)} %get-tuple-element.19), channel_id=1, source_target_pairs={{0,8},{8,0},{16,24},{24,16},{32,40},{40,32},{48,56},{56,48},{64,72... | collective-permute-start | bytes 1179656 | tf_op jit(solution)/shard_map/ppermute | solution.py:249
  60.3 17.5 %all-to-all-start.1 = ((f32[16,48,128]{2,1,0:T(8,128)}), f32[16,48,128]{2,1,0:T(8,128)S(1)}, u32[]{:S(2)}, u32[]{:S(2)}) async-start(f32[16,48,128]{2,1,0:T(8,128)} %broadcast_in_dim.25), calls=%async_computation.1 | async-start | bytes 786432 | tf_op jit(solution)/shard_map/all_to_all | solution.py:252
  63.8 14.0 %collective-permute-start.7 = (f32[1,8,128]{2,1,0:T(8,128)S(1)}, f32[1,8,128]{2,1,0:T(8,128)S(1)}, u32[]{:S(2)}, u32[]{:S(2)}) collective-permute-start(f32[1,8,128]{2,1,0:T(8,128)S(1)} %get-tuple-element.26), channel_id=1, source_target_pairs={{0,1},{1,0},{2,3},{3,2},{4,5},{5,4},{6,7},{7,6},{8,9},{9,8},{10,11... | collective-permute-start | bytes 12296 | tf_op jit(solution)/shard_map/ppermute | solution.py:250
  77.8 22.7 %collective-permute-start.6 = (f32[16,48,128]{2,1,0:T(8,128)S(1)}, f32[16,48,128]{2,1,0:T(8,128)S(1)}, u32[]{:S(2)}, u32[]{:S(2)}) collective-permute-start(f32[16,48,128]{2,1,0:T(8,128)S(1)} %all-to-all-done.1.field_ref), channel_id=1, source_target_pairs={{0,8},{8,0},{16,24},{24,16},{32,40},{40,32},{48,56},{56,48},{64,72... | collective-permute-start | bytes 1179656 | tf_op jit(solution)/shard_map/ppermute | solution.py:249
  77.8 5.2 %collective-permute-start.8 = (f32[2,8,128]{2,1,0:T(8,128)S(1)}, f32[2,8,128]{2,1,0:T(8,128)S(1)}, u32[]{:S(2)}, u32[]{:S(2)}) collective-permute-start(f32[2,8,128]{2,1,0:T(8,128)S(1)} %pad_maximum_fusion.5), channel_id=1, source_target_pairs={{0,2},{1,3},{2,0},{3,1},{4,6},{5,7},{6,4},{7,5},{8,10},{9,11},{10,... | collective-permute-start | bytes 24584 | tf_op jit(solution)/shard_map/ppermute | solution.py:250
  83.1 5.2 %collective-permute-start.9 = (f32[4,8,128]{2,1,0:T(8,128)S(1)}, f32[4,8,128]{2,1,0:T(8,128)S(1)}, u32[]{:S(2)}, u32[]{:S(2)}) collective-permute-start(f32[4,8,128]{2,1,0:T(8,128)S(1)} %pad_maximum_fusion.3), channel_id=1, source_target_pairs={{0,4},{1,5},{2,6},{3,7},{4,0},{5,1},{6,2},{7,3},{8,12},{9,13},{10,... | collective-permute-start | bytes 49160 | tf_op jit(solution)/shard_map/ppermute | solution.py:250
  131.9 2.5 %collective-permute-start.10 = (f32[16,48,128]{2,1,0:T(8,128)S(1)}, f32[16,48,128]{2,1,0:T(8,128)S(1)}, u32[]{:S(2)}, u32[]{:S(2)}) collective-permute-start(f32[16,48,128]{2,1,0:T(8,128)S(1)} %all_to_all.27.field_ref), channel_id=1, source_target_pairs={{0,8},{8,0},{16,24},{24,16},{32,40},{40,32},{48,56},{56,48},{64,72... | collective-permute-start | bytes 1179656 | tf_op jit(solution)/shard_map/ppermute | solution.py:249

commit v3 on v2

v3 whole, which is shorter than its diff:
```python
import functools
import math

import jax
import jax.numpy as jnp
from jax import lax
from jax.experimental import pallas as pl
from jax.experimental.pallas import tpu as pltpu
from jax.sharding import PartitionSpec as P


TILE = 128
RADIUS = 0.15
KERNEL_GAIN = 3200.0
RHS_GAIN = 28.0
LOWER_EDGE = 1.0
UPPER_EDGE = 4.0

SCALE = 4.0 / RADIUS
PHI = 1.0 / 256.0
FAR = 4096.0
DEPTH = 128
GRANT = 20 << 20


def split3(x):
    one = x.astype(jnp.bfloat16).astype(jnp.float32)
    rest = x - one
    two = rest.astype(jnp.bfloat16).astype(jnp.float32)
    return one, two, rest - two


def padded(points):
    fill = jnp.full((8 - points.shape[0], points.shape[1]), 0.5, jnp.float32)
    return jnp.concatenate([points, fill], axis=0)


def features(points, target, extra=None):
    count = points.shape[1]
    centred = (points - 0.5) * SCALE
    norm = jnp.sum(centred * centred, axis=0, keepdims=True)
    n1, n2, n3 = split3(jnp.broadcast_to(norm, (8, count)))
    row = lax.broadcasted_iota(jnp.int32, (8, count), 0)
    one, zero = jnp.ones_like(n1), jnp.zeros_like(n1)
    if target:
        c1, c2, c3 = split3(-2.0 * centred)
        tail = jnp.where(row < 3, one, jnp.where(row == 3, n1, jnp.where(row == 4, n2, jnp.where(row == 5, n3, zero))))
        groups = [c1, c2, c1, c2, c3, c1, tail]
    else:
        c1, c2, c3 = split3(centred)
        tail = jnp.where(row == 0, n1, jnp.where(row == 1, n2, jnp.where(row == 2, n3, jnp.where(row < 6, one, zero))))
        groups = [c1, c1, c2, c2, c1, c3, tail]
    used = 8 * len(groups)
    if extra is not None:
        groups.append(extra)
        used += extra.shape[0]
    groups.append(jnp.zeros((DEPTH - used, count), jnp.float32))
    return jnp.concatenate(groups, axis=0)


def profile(d2):
    d2 = jnp.maximum(d2, 1e-12)
    w = jnp.maximum(4.0 - d2 * lax.rsqrt(d2), 0.0)
    square = w * w
    return (square * square) * (5.0 - w)


def stage_kernel(vol_ref, adj_ref, mask_ref, feat_ref, weights_ref, absent_ref, near_ref, held_ref, sem_ref):
    copies = [
        pltpu.make_async_copy(vol_ref, near_ref, sem_ref.at[0]),
        pltpu.make_async_copy(mask_ref, held_ref, sem_ref.at[1]),
        pltpu.make_async_copy(adj_ref, weights_ref, sem_ref.at[2]),
    ]
    for copy in copies:
        copy.start()
    for copy in copies:
        copy.wait()
    rows = vol_ref.shape[1]
    tiles = rows // TILE
    tile = lax.broadcasted_iota(jnp.int32, (tiles, rows), 0)
    place = lax.broadcasted_iota(jnp.int32, (tiles, rows), 1) // TILE
    onehot = jnp.where(tile == place, 1.0, 0.0)
    feat_ref[...] = features(padded(near_ref[...]), False, onehot).T.astype(jnp.bfloat16)
    absent_ref[...] = (1 - held_ref[...]).astype(jnp.float32)


def stage(vol, adj, mask):
    return pl.pallas_call(
        stage_kernel,
        in_specs=[pl.BlockSpec(memory_space=pltpu.HBM)] * 3,
        out_specs=[pl.BlockSpec(memory_space=pltpu.VMEM)] * 3,
        out_shape=(
            jax.ShapeDtypeStruct((vol.shape[1], DEPTH), jnp.bfloat16),
            jax.ShapeDtypeStruct(adj.shape, jnp.bfloat16),
            jax.ShapeDtypeStruct(mask.shape, jnp.float32),
        ),
        scratch_shapes=[
            pltpu.VMEM(vol.shape, jnp.float32),
            pltpu.VMEM(mask.shape, jnp.int32),
            pltpu.SemaphoreType.DMA((3,)),
        ],
        name="stage",
        compiler_params=pltpu.CompilerParams(vmem_limit_bytes=GRANT),
        cost_estimate=pl.CostEstimate(flops=1 << 20, bytes_accessed=2 << 20, transcendentals=0),
    )(*[pltpu.with_memory_space_constraint(x, pltpu.HBM) for x in (vol, adj, mask)])


def coupling_kernel(base, spot_ref, feat_ref, adj_ref, absent_ref, cols_ref, *refs):
    rows = feat_ref.shape[0]
    width = cols_ref.shape[2]
    far = (base + pl.program_id(0)) ^ spot_ref[1]
    lower = (spot_ref[0] >> 1) & 1

    tile = lax.broadcasted_iota(jnp.int32, (absent_ref.shape[1], width), 0)
    piece = lax.broadcasted_iota(jnp.int32, (absent_ref.shape[1], width), 1) // TILE
    swapped = (piece % 2) * 2 + piece // 2
    pick = jnp.where(tile == 4 * far + (swapped ^ spot_ref[0]), 1.0, 0.0).astype(jnp.bfloat16)
    barred = FAR * jnp.dot(absent_ref[...].astype(jnp.bfloat16), pick, preferred_element_type=jnp.float32)
    target = features(cols_ref[0], True, barred).astype(jnp.bfloat16)

    half = width // 2
    step = 512
    for side, out_ref in enumerate(refs[-2:]):
        total = jnp.zeros((adj_ref.shape[0], half), jnp.float32)
        for start in range(0, rows, step):
            d2 = jnp.dot(
                feat_ref[start:start + step, :],
                target[:, side * half:(side + 1) * half],
                preferred_element_type=jnp.float32,
            )
            values = profile(d2).astype(jnp.bfloat16)
            total += jnp.dot(adj_ref[:, start:start + step], values, preferred_element_type=jnp.float32)
        out_ref[lower] = total[:, :TILE]
        out_ref[1 - lower] = total[:, TILE:]


def coupling(base, blocks, spot, staged, cols, earlier=()):
    feat, adj, absent = staged
    count, axes, width = cols.shape
    objs = adj.shape[0]
    whole = lambda shape: pl.BlockSpec(shape, lambda i, s: (0,) * len(shape))
    out = jax.ShapeDtypeStruct((2 * blocks, objs, TILE), jnp.float32)
    place = pl.BlockSpec((2, objs, TILE), lambda i, s: ((base + i) ^ s[1], 0, 0))
    return pl.pallas_call(
        functools.partial(coupling_kernel, base),
        grid_spec=pltpu.PrefetchScalarGridSpec(
            num_scalar_prefetch=1,
            grid=(count,),
            in_specs=[
                whole(feat.shape),
                whole(adj.shape),
                whole(absent.shape),
                pl.BlockSpec((1, axes, width), lambda i, s: (i, 0, 0)),
            ] + [pl.BlockSpec(memory_space=pl.ANY)] * len(earlier),
            out_specs=[place] * 2,
        ),
        out_shape=(out, out),
        input_output_aliases={5 + i: i for i in range(len(earlier))},
        compiler_params=pltpu.CompilerParams(vmem_limit_bytes=GRANT),
        cost_estimate=pl.CostEstimate(
            flops=20 * feat.shape[0] * count * width, bytes_accessed=2 << 20, transcendentals=0
        ),
    )(spot, feat, adj, absent, cols, *earlier)


def gram_kernel(spot_ref, points_ref, rows_ref, out_ref, feat_ref, source_ref):
    lower = (spot_ref[0] >> 1) & 1

    @pl.when((pl.program_id(0) == 0) & (pl.program_id(1) == 0))
    def _():
        slots = [2 * ((j // 2) ^ spot_ref[2]) + ((j % 2) ^ lower) for j in range(rows_ref.shape[0])]
        points = jnp.concatenate([rows_ref[slot] for slot in slots], axis=1)
        whole = features(points, True).astype(jnp.bfloat16)
        part = feat_ref.shape[2]
        for j in range(feat_ref.shape[0]):
            feat_ref[j] = whole[:, j * part:(j + 1) * part]

    @pl.when(pl.program_id(1) == 0)
    def _():
        odd = spot_ref[1] & 1
        pair = (points_ref[odd], points_ref[1 - odd])
        pieces = [part[:, 2 * side * TILE:(2 * side + 1) * TILE] for side in range(2) for part in pair]
        source_ref[...] = features(jnp.concatenate(pieces, axis=1), False).T.astype(jnp.bfloat16)

    source = source_ref[...]
    width = out_ref.shape[3]
    step = 256
    for start in range(0, width, step):
        d2 = jnp.dot(
            source, feat_ref[pl.program_id(1), :, start:start + step], preferred_element_type=jnp.float32
        )
        values = profile(d2).astype(jnp.bfloat16)
        out_ref[0, 0, :, start:start + step] = values[:2 * TILE]
        out_ref[1, 0, :, start:start + step] = values[2 * TILE:]


def gram(spot, points, rows):
    count, axes, lanes = points.shape
    width = rows.shape[0] * rows.shape[2]
    parts = 2
    return pl.pallas_call(
        gram_kernel,
        grid_spec=pltpu.PrefetchScalarGridSpec(
            num_scalar_prefetch=1,
            grid=(count // 2, parts),
            in_specs=[
                pl.BlockSpec((2, axes, lanes), lambda i, k, s: (i, 0, 0)),
                pl.BlockSpec(rows.shape, lambda i, k, s: (0, 0, 0)),
            ],
            out_specs=pl.BlockSpec((2, 1, 2 * TILE, width // parts), lambda i, k, s: (0, i ^ (s[1] >> 1), 0, k)),
            scratch_shapes=[
                pltpu.VMEM((parts, DEPTH, width // parts), jnp.bfloat16),
                pltpu.VMEM((4 * TILE, DEPTH), jnp.bfloat16),
            ],
        ),
        out_shape=pltpu.HBM((2, count // 2, 2 * TILE, width), jnp.bfloat16),
        name="gram",
        compiler_params=pltpu.CompilerParams(vmem_limit_bytes=GRANT),
        cost_estimate=pl.CostEstimate(flops=40 * count * TILE * width, bytes_accessed=8 << 20, transcendentals=0),
    )(spot, points, rows)


def mix_kernel(fresh, side, field_ref, gram_ref, *refs):
    if fresh:
        out_ref, held_ref, sem_ref = refs[-3:]
    else:
        out_ref, held_ref = refs[-1], gram_ref
    blocks, _, width = held_ref.shape
    objs = field_ref.shape[1]
    copies = []
    if fresh:
        copies = [pltpu.make_async_copy(gram_ref.at[side, z], held_ref.at[z], sem_ref.at[z]) for z in range(blocks)]
    for copy in copies:
        copy.start()
    total = jnp.zeros((2 * objs, width), jnp.float32)
    for z in range(blocks):
        field = jnp.concatenate([field_ref[2 * z], field_ref[2 * z + 1]], axis=1)
        high = field.astype(jnp.bfloat16).astype(jnp.float32)
        both = jnp.concatenate([high, field - high], axis=0).astype(jnp.bfloat16)
        if fresh:
            copies[z].wait()
        total += jnp.dot(both, held_ref[z], preferred_element_type=jnp.float32)
    for j in range(out_ref.shape[0]):
        part = total[:objs, j * TILE:(j + 1) * TILE] + total[objs:, j * TILE:(j + 1) * TILE]
        out_ref[j] = part if side == 0 else part + refs[0][j]


def mix(side, field, block, earlier=()):
    fresh = block.ndim == 4
    objs = field.shape[1]
    blocks, depth, width = block.shape[-3:]
    parts = width // TILE
    vmem = pl.BlockSpec(memory_space=pltpu.VMEM)
    out = jax.ShapeDtypeStruct((parts, objs, TILE), jnp.float32)
    place = pltpu.HBM if fresh else pltpu.VMEM
    result = pl.pallas_call(
        functools.partial(mix_kernel, fresh, side),
        in_specs=[vmem, pl.BlockSpec(memory_space=place)] + [vmem] * len(earlier),
        out_specs=[vmem, vmem] if fresh else vmem,
        out_shape=(out, pltpu.VMEM((blocks, depth, width), jnp.bfloat16)) if fresh else out,
        scratch_shapes=[pltpu.SemaphoreType.DMA((blocks,))] if fresh else [],
        name="mix",
        compiler_params=pltpu.CompilerParams(vmem_limit_bytes=GRANT),
        cost_estimate=pl.CostEstimate(flops=4 * objs * blocks * depth * width, bytes_accessed=5 << 20, transcendentals=0),
    )(field, pltpu.with_memory_space_constraint(block, place), *earlier)
    return result if fresh else (result, block)


def body(n_wide, n_narrow, vol_points, vol_adjoint, surf_points, tile_mask):
    far = n_wide // 4
    chips = [[2 * k + core for k in range(2 * far)] for core in range(2)]
    column = [[4 * z + r for z in range(far)] for r in range(4)]
    plane = [
        [n * n_wide + 4 * z + 2 * y + core for n in range(n_narrow) for y in range(2)]
        for z in range(far)
        for core in range(2)
    ]
    swap = lambda x, bit: lax.ppermute(x, "wide", [(i, i ^ bit) for i in range(n_wide)])
    side = lambda x, bit: lax.ppermute(x, "narrow", [(i, i ^ bit) for i in range(n_narrow)])
    repeat = lambda x, count: jnp.broadcast_to(x[None], (count,) + x.shape)
    join = lambda x, y: jnp.concatenate([x, y], axis=0)

    wide = lax.axis_index("wide").astype(jnp.int32)
    spot = jnp.stack([wide & 3, wide >> 2, lax.axis_index("narrow").astype(jnp.int32)])
    own = jnp.pad(surf_points, ((0, 5), (0, 0)), constant_values=0.5)
    staged = stage(vol_points, vol_adjoint, tile_mask)
    across = swap(own, 2)
    pair = jnp.concatenate([own, across], axis=1)
    rows = jnp.stack([own, across])
    quad = jnp.concatenate([pair, swap(pair, 1)], axis=1)[None]
    rows = join(rows, side(rows, 1))
    two = join(quad, swap(quad, 4))
    rows = join(rows, side(rows, 2))
    four = join(two, swap(two, 8))
    rows = join(rows, side(rows, 4))
    next_four = swap(four, 16)
    sums = coupling(0, far, spot, staged, four)
    keep, send = coupling(4, far, spot, staged, next_four, sums)
    got = swap(send, 1)
    block = gram(spot, join(four, next_four), rows)
    parts = lax.all_to_all(keep + got, "wide", 0, 0, axis_index_groups=chips, tiled=True)

    total_volume = vol_points.shape[1] * n_wide
    total_surface = surf_points.shape[1] * n_wide * n_narrow
    centre = (LOWER_EDGE + UPPER_EDGE) / 2.0
    half_width = (UPPER_EDGE - LOWER_EDGE) / 2.0
    sigma = centre / half_width
    rho_zero = 1.0 / sigma
    rho_one = 1.0 / (2.0 * sigma - rho_zero)
    gain = KERNEL_GAIN / total_surface * PHI

    def mixed(field, zero, one):
        mine = lax.all_to_all(repeat(field, far), "wide", 0, 0, axis_index_groups=column, tiled=True)
        other = swap(mine, 1)
        partial, zero = mix(0, mine, zero)
        partial, one = mix(1, other, one, (partial,))
        total = add_up(
            lax.all_to_all(partial, ("narrow", "wide"), 0, 0, axis_index_groups=plane, tiled=True)
        )
        return total, zero, one

    rhs = add_up(parts) * (RHS_GAIN / math.sqrt(total_volume) * PHI)
    first = rhs / centre
    product, zero, one = mixed(first, block, block)
    near = rhs - (first + gain * product)
    update = rho_one * rho_zero * first + 2.0 * rho_one / half_width * near
    solution = first + update
    product, _, _ = mixed(update, zero, one)
    residual = near - (update + gain * product)
    return (solution, residual)


def add_up(parts):
    total = parts[0]
    for k in range(1, parts.shape[0]):
        total = total + parts[k]
    return total


def solution(mesh):
    return jax.shard_map(
        functools.partial(body, mesh.shape["wide"], mesh.shape["narrow"]),
        mesh=mesh,
        in_specs=(
            P(None, "wide"),
            P(None, "wide"),
            P(None, ("narrow", "wide")),
            P("wide", "narrow"),
        ),
        out_specs=(P(None, ("narrow", "wide")), P(None, ("narrow", "wide"))),
        check_vma=False,
    )
```

time: 150 us -> 139 us (0.927)
  blocking collectives: 59.4 us -> 44.6 us
  starting transfers between devices: 22.9 us -> 27.1 us
  Pallas kernels: 37.4 us -> 33.4 us
  waiting for transfers between devices: 26.1 us -> 28 us
    all_to_all x4 -> x3, blocking collectives: 59.4 us -> 44.6 us  [the longest x2 28.4 us: mixed(): lax.all_to_all(partial, ('narrow', 'wide'), 0, 0, axis_index_groups=plane...]
    all_to_all x1 -> x2, starting transfers between devices: 3.55 us -> 7.68 us  [the longest x1 4.29 us: body(): lax.all_to_all(keep + got, 'wide', 0, 0, axis_index_groups=chips, tiled=T...]
    pallas_call x4, Pallas kernels: 9.76 us -> 6.63 us  [mix(): pl.pallas_call(functools.partial(mix_kernel, fresh, side), in_specs=[vmem...]
    all_to_all x1 -> x2, waiting for transfers between devices: 13.4 us -> 15.9 us  [the longest x1 14.3 us: body(): lax.all_to_all(keep + got, 'wide', 0, 0, axis_index_groups=chips, tiled=T...]
    pallas_call x3 -> x2, Pallas kernels: 16.6 us -> 16.1 us  [coupling(): pl.pallas_call(functools.partial(coupling_kernel, base), grid_spec=pltpu....]
  transfers between devices with their start and end apart: 12 -> 13, of which waited for: 8 -> 10; matrix products, arithmetic and copies ran while one was open for 0% -> 1% of each run, Pallas kernels for 16% -> 16%
where the time goes in v3:
time: 139 us; the launch traced here: 137 us
  blocking collectives  44.6 us (32%)
  Pallas kernels  33.4 us (24%)
  waiting for transfers between devices  28 us (20%)
  starting transfers between devices  27.1 us (19%)
  other arithmetic  1.62 us (1%)
  local copies, waits for them, and re-layouts  1.48 us (1%)
    all_to_all x2, blocking collectives, mixed(): lax.all_to_all(partial, ('narrow', 'wide'), 0, 0, axis_index_groups=plane...  28.4 us
    all_to_all x1, blocking collectives, mixed(): lax.all_to_all(repeat(field, far), 'wide', 0, 0, axis_index_groups=column...  16.2 us
    pallas_call x2, Pallas kernels, coupling(): pl.pallas_call(functools.partial(coupling_kernel, base), grid_spec=pltpu....  16.1 us
    all_to_all x1, waiting for transfers between devices, body(): lax.all_to_all(keep + got, 'wide', 0, 0, axis_index_groups=chips, tiled=T...  14.3 us
    ppermute x8, starting transfers between devices, body(): lax.ppermute(x, 'wide', [(i, i ^ bit) for i in range(n_wide)])  13.6 us
    pallas_call x1, Pallas kernels, gram(): pl.pallas_call(gram_kernel, grid_spec=pltpu.PrefetchScalarGridSpec(num_sc...  9.48 us
    ppermute x8, waiting for transfers between devices, body(): lax.ppermute(x, 'wide', [(i, i ^ bit) for i in range(n_wide)])  8.07 us
    pallas_call x4, Pallas kernels, mix(): pl.pallas_call(functools.partial(mix_kernel, fresh, side), in_specs=[vmem...  6.63 us
  transfers between devices with their start and end apart: 13, of which 10 were waited for; matrix products, arithmetic and copies ran while one was open for 1% of the time, Pallas kernels for 16%

profile of v3, /device:TPU:2, one launch (start us, length us, event | category | flops | bytes accessed | tf_op | source)
XLA Modules:
  0.0 136.9 jit_solution(18068766716829213067)
XLA Ops:
  0.6 0.0 copy-start
  0.6 0.8 pad_bitcast_fusion
  1.4 1.6 %collective-permute-start = (f32[8,128]{1,0:T(8,128)S(1)}, f32[8,128]{1,0:T(8,128)S(1)}, u32[]{:S(2)}, u32[]{:S(2)}) collective-permute-start(f32[8,128]{1,0:T(8,128)S(1)} %get-tuple-element.31), channel_id=1, source_target_pairs={{0,16},{8,24},{16,0},{24,8},{32,48},{40,56},{48,32},{56,40},{64,80... | collective-permute-start | bytes 12296 | tf_op jit(solution)/shard_map/ppermute | solution.py:278
  3.0 2.0 %collective-permute-done = f32[8,128]{1,0:T(8,128)S(1)} collective-permute-done((f32[8,128]{1,0:T(8,128)S(1)}, f32[8,128]{1,0:T(8,128)S(1)}, u32[]{:S(2)}, u32[]{:S(2)}) %collective-permute-start) | collective-permute-done | bytes 4128 | tf_op jit(solution)/shard_map/ppermute | solution.py:278
  5.0 0.0 collective-permute-start.1
  5.0 1.2 collective-permute-done.1
  6.2 1.9 %collective-permute-start.2 = (f32[1,8,512]{2,1,0:T(8,128)S(1)}, f32[1,8,512]{2,1,0:T(8,128)S(1)}, u32[]{:S(2)}, u32[]{:S(2)}) collective-permute-start(f32[1,8,512]{2,1,0:T(8,128)S(1)} %maximum_bitcast_fusion), channel_id=1, source_target_pairs={{0,32},{8,40},{16,48},{24,56},{32,0},{40,8},{48,16},{56,24},{64,96... | collective-permute-start | bytes 49160 | tf_op jit(solution)/shard_map/ppermute | solution.py:278
  8.1 1.8 %collective-permute-done.2 = f32[1,8,512]{2,1,0:T(8,128)S(1)} collective-permute-done((f32[1,8,512]{2,1,0:T(8,128)S(1)}, f32[1,8,512]{2,1,0:T(8,128)S(1)}, u32[]{:S(2)}, u32[]{:S(2)}) %collective-permute-start.2) | collective-permute-done | bytes 16416 | tf_op jit(solution)/shard_map/ppermute | solution.py:278
  9.9 3.3 %collective-permute-start.3 = (f32[2,8,512]{2,1,0:T(8,128)S(1)}, f32[2,8,512]{2,1,0:T(8,128)S(1)}, u32[]{:S(2)}, u32[]{:S(2)}) collective-permute-start(f32[2,8,512]{2,1,0:T(8,128)S(1)} %pad_maximum_fusion.2), channel_id=1, source_target_pairs={{0,64},{8,72},{16,80},{24,88},{32,96},{40,104},{48,112},{56,120},{... | collective-permute-start | bytes 98312 | tf_op jit(solution)/shard_map/ppermute | solution.py:278
  13.2 1.2 stage.1
  14.4 0.7 collective-permute-done.3
  15.1 6.8 %collective-permute-start.4 = (f32[4,8,512]{2,1,0:T(8,128)S(1)}, f32[4,8,512]{2,1,0:T(8,128)S(1)}, u32[]{:S(2)}, u32[]{:S(2)}) collective-permute-start(f32[4,8,512]{2,1,0:T(8,128)S(1)} %pad_maximum_fusion.1.cols_ref), channel_id=1, source_target_pairs={{0,128},{8,136},{16,144},{24,152},{32,160},{40,168},{48,176},{56,1... | collective-permute-start | bytes 196616 | tf_op jit(solution)/shard_map/ppermute | solution.py:278
  22.0 0.1 pad_add_fusion.spot_ref
  22.0 8.0 %shard_map.59 = (f32[16,48,128]{2,1,0:T(8,128)S(1)}, f32[16,48,128]{2,1,0:T(8,128)S(1)}) custom-call(s32[3]{0:T(128)S(1)} %pad_add_fusion.spot_ref, bf16[2048,128]{1,0:T(8,128)(2,1)S(1)} %get-tuple-element.13.feat_ref, bf16[48,2048]{1,0:T(8,128)(2,1)S(1)} %get-tuple-element.14.adj_ref, f32[16,32]{1,0:T(8,128)S(1)} %get-tuple-element.15.absent_ref, ...), custom_call_target="tpu_custom_call" | custom-call | flops 83886080 | bytes 2097152 | tf_op jit(solution)/shard_map/pallas_call | solution.py:144
  30.1 0.0 collective-permute-done.4.cols_ref
  30.1 8.0 %shard_map.60 = (f32[16,48,128]{2,1,0:T(8,128)S(1)}, f32[16,48,128]{2,1,0:T(8,128)S(1)}) custom-call(s32[3]{0:T(128)S(1)} %pad_add_fusion.spot_ref, bf16[2048,128]{1,0:T(8,128)(2,1)S(1)} %get-tuple-element.13.feat_ref, bf16[48,2048]{1,0:T(8,128)(2,1)S(1)} %get-tuple-element.14.adj_ref, ...), custom_call_target="tpu_custom_call", output_to_operand_aliasing={{0}: (5, {}), {1}: (6, {})} | custom-call | flops 83886080 | bytes 2097152 | tf_op jit(solution)/shard_map/pallas_call | solution.py:144
  38.1 0.0 collective-permute-start.5
  38.2 1.7 %collective-permute-done.5 = f32[16,48,128]{2,1,0:T(8,128)S(1)} collective-permute-done((f32[16,48,128]{2,1,0:T(8,128)S(1)}, f32[16,48,128]{2,1,0:T(8,128)S(1)}, u32[]{:S(2)}, u32[]{:S(2)}) %collective-permute-start.5) | collective-permute-done | bytes 393248 | tf_op jit(solution)/shard_map/ppermute | solution.py:278
  39.9 0.8 add.265
  40.7 4.3 %all-to-all-start = ((f32[16,48,128]{2,1,0:T(8,128)}), f32[16,48,128]{2,1,0:T(8,128)S(1)}, u32[]{:S(2)}, u32[]{:S(2)}) async-start(f32[16,48,128]{2,1,0:T(8,128)} %add.265), calls=%async_computation | async-start | bytes 786432 | tf_op jit(solution)/shard_map/all_to_all | solution.py:301
  45.0 0.0 copy-done
  45.0 0.6 collective-permute-start.7
  45.6 14.3 %all-to-all-done = f32[16,48,128]{2,1,0:T(8,128)S(1)} async-done(((f32[16,48,128]{2,1,0:T(8,128)}), f32[16,48,128]{2,1,0:T(8,128)S(1)}, u32[]{:S(2)}, u32[]{:S(2)}) %all-to-all-start) | async-done | bytes 393248 | tf_op jit(solution)/shard_map/all_to_all | solution.py:301
  60.0 0.7 broadcast_in_dim.21
  60.7 3.4 %all-to-all-start.1 = ((f32[8,48,128]{2,1,0:T(8,128)}), f32[8,48,128]{2,1,0:T(8,128)S(1)}, u32[]{:S(2)}, u32[]{:S(2)}) async-start(f32[8,48,128]{2,1,0:T(8,128)} %broadcast_in_dim.21), calls=%async_computation.1 | async-start | bytes 393216 | tf_op jit(solution)/shard_map/all_to_all | solution.py:313
  64.1 0.0 collective-permute-done.7
  64.1 2.2 %collective-permute-start.8 = (f32[4,8,128]{2,1,0:T(8,128)S(1)}, f32[4,8,128]{2,1,0:T(8,128)S(1)}, u32[]{:S(2)}, u32[]{:S(2)}) collective-permute-start(f32[4,8,128]{2,1,0:T(8,128)S(1)} %pad_maximum_fusion.4), channel_id=1, source_target_pairs={{0,2},{1,3},{2,0},{3,1},{4,6},{5,7},{6,4},{7,5},{8,10},{9,11},{10,... | collective-permute-start | bytes 49160 | tf_op jit(solution)/shard_map/ppermute | solution.py:279
  66.3 3.1 %collective-permute-done.8 = f32[4,8,128]{2,1,0:T(8,128)S(1)} collective-permute-done((f32[4,8,128]{2,1,0:T(8,128)S(1)}, f32[4,8,128]{2,1,0:T(8,128)S(1)}, u32[]{:S(2)}, u32[]{:S(2)}) %collective-permute-start.8) | collective-permute-done | bytes 16416 | tf_op jit(solution)/shard_map/ppermute | solution.py:279
  69.4 2.9 %collective-permute-start.9 = (f32[8,8,128]{2,1,0:T(8,128)S(1)}, f32[8,8,128]{2,1,0:T(8,128)S(1)}, u32[]{:S(2)}, u32[]{:S(2)}) collective-permute-start(f32[8,8,128]{2,1,0:T(8,128)S(1)} %pad_maximum_fusion.3), channel_id=1, source_target_pairs={{0,4},{1,5},{2,6},{3,7},{4,0},{5,1},{6,2},{7,3},{8,12},{9,13},{10,... | collective-permute-start | bytes 98312 | tf_op jit(solution)/shard_map/ppermute | solution.py:279
  72.3 1.6 %all-to-all-done.1.field_ref = f32[8,48,128]{2,1,0:T(8,128)S(1)} async-done(((f32[8,48,128]{2,1,0:T(8,128)}), f32[8,48,128]{2,1,0:T(8,128)S(1)}, u32[]{:S(2)}, u32[]{:S(2)}) %all-to-all-start.1) | async-done | bytes 196640 | tf_op jit(solution)/shard_map/all_to_all | solution.py:313
  74.0 0.0 collective-permute-start.6
  74.0 0.9 collective-permute-done.9
  74.9 9.5 %gram.1.gram_ref = bf16[2,4,256,2048]{3,2,1,0:T(8,128)(2,1)} custom-call(s32[3]{0:T(128)S(1)} %pad_add_fusion.spot_ref, f32[8,8,512]{2,1,0:T(8,128)S(1)} %pad_maximum_fusion.points_ref, f32[16,8,128]{2,1,0:T(8,128)S(1)} %constant_dynamic-update-slice_fusion.rows_ref), custom_call_target="tpu_custom_call" | custom-call | flops 83886080 | bytes 8388608 | tf_op jit(solution)/shard_map/gram/pallas_call | solution.py:201
  84.3 2.5 %mix.4 = (f32[16,48,128]{2,1,0:T(8,128)S(1)}, bf16[4,256,2048]{2,1,0:T(8,128)(2,1)S(1)}) custom-call(f32[8,48,128]{2,1,0:T(8,128)S(1)} %all-to-all-done.1.field_ref, bf16[2,4,256,2048]{3,2,1,0:T(8,128)(2,1)} %gram.1.gram_ref), custom_call_target="tpu_custom_call" | custom-call | flops 402653184 | bytes 5242880 | tf_op jit(solution)/shard_map/mix/pallas_call | solution.py:256
  86.9 0.0 collective-permute-done.6.field_ref
  86.9 2.5 %mix.5 = (f32[16,48,128]{2,1,0:T(8,128)S(1)}, bf16[4,256,2048]{2,1,0:T(8,128)(2,1)S(1)}) custom-call(f32[8,48,128]{2,1,0:T(8,128)S(1)} %collective-permute-done.6.field_ref, bf16[2,4,256,2048]{3,2,1,0:T(8,128)(2,1)} %gram.1.gram_ref, f32[16,48,128]{2,1,0:T(8,128)S(1)} %get-tuple-element.20.refs_0_), custom_call_target="tpu_custom_call" | custom-call | flops 402653184 | bytes 5242880 | tf_op jit(solution)/shard_map/mix/pallas_call | solution.py:256
  89.4 14.7 %all_to_all.25 = f32[16,48,128]{2,1,0:T(8,128)S(1)} all-to-all(f32[16,48,128]{2,1,0:T(8,128)S(1)} %get-tuple-element.21), channel_id=1, replica_groups={{0,16,1,17,2,18,3,19,4,20,5,21,6,22,7,23},{8,24,9,25,10,26,11,27,12,28,..., dimensions={0} | all-to-all | bytes 786432 | tf_op jit(solution)/shard_map/all_to_all | solution.py:318
  104.2 16.2 %all_to_all.26.field_ref = f32[8,48,128]{2,1,0:T(8,128)S(1)} all-to-all(f32[8,48,128]{2,1,0:T(8,128)S(1)} %broadcast_in_dim.23), channel_id=1, replica_groups={{0,32,64,96,128,160,192,224},{8,40,72,104,136,168,200,232},{16,48,80,11..., dimensions={0} | all-to-all | bytes 393216 | tf_op jit(solution)/shard_map/all_to_all | solution.py:313
  120.4 0.0 collective-permute-start.10
  120.4 0.8 mix.6.refs_0_
  121.2 0.6 collective-permute-done.10.field_ref
  121.8 0.8 mix.7
  122.6 13.6 %all_to_all.27 = f32[16,48,128]{2,1,0:T(8,128)S(1)} all-to-all(f32[16,48,128]{2,1,0:T(8,128)S(1)} %mix.7), channel_id=1, replica_groups={{0,16,1,17,2,18,3,19,4,20,5,21,6,22,7,23},{8,24,9,25,10,26,11,27,12,28,..., dimensions={0} | all-to-all | bytes 786432 | tf_op jit(solution)/shard_map/all_to_all | solution.py:318
  136.3 0.6 fusion.3
  (16 shorter events, 0.1 us)
Async XLA Ops:
  0.6 44.3 %copy-start = (f32[3,128]{1,0:T(4,128)S(1)}, f32[3,128]{1,0:T(4,128)}, u32[]{:S(2)}) copy-start(f32[3,128]{1,0:T(4,128)} %param.6) | copy-start | bytes 4612
  1.4 3.6 %collective-permute-start = (f32[8,128]{1,0:T(8,128)S(1)}, f32[8,128]{1,0:T(8,128)S(1)}, u32[]{:S(2)}, u32[]{:S(2)}) collective-permute-start(f32[8,128]{1,0:T(8,128)S(1)} %get-tuple-element.31), channel_id=1, source_target_pairs={{0,16},{8,24},{16,0},{24,8},{32,48},{40,56},{48,32},{56,40},{64,80... | collective-permute-start | bytes 12296 | tf_op jit(solution)/shard_map/ppermute | solution.py:278
  5.0 1.2 collective-permute-start.1
  6.2 3.7 %collective-permute-start.2 = (f32[1,8,512]{2,1,0:T(8,128)S(1)}, f32[1,8,512]{2,1,0:T(8,128)S(1)}, u32[]{:S(2)}, u32[]{:S(2)}) collective-permute-start(f32[1,8,512]{2,1,0:T(8,128)S(1)} %maximum_bitcast_fusion), channel_id=1, source_target_pairs={{0,32},{8,40},{16,48},{24,56},{32,0},{40,8},{48,16},{56,24},{64,96... | collective-permute-start | bytes 49160 | tf_op jit(solution)/shard_map/ppermute | solution.py:278
  9.9 5.2 %collective-permute-start.3 = (f32[2,8,512]{2,1,0:T(8,128)S(1)}, f32[2,8,512]{2,1,0:T(8,128)S(1)}, u32[]{:S(2)}, u32[]{:S(2)}) collective-permute-start(f32[2,8,512]{2,1,0:T(8,128)S(1)} %pad_maximum_fusion.2), channel_id=1, source_target_pairs={{0,64},{8,72},{16,80},{24,88},{32,96},{40,104},{48,112},{56,120},{... | collective-permute-start | bytes 98312 | tf_op jit(solution)/shard_map/ppermute | solution.py:278
  15.1 15.0 %collective-permute-start.4 = (f32[4,8,512]{2,1,0:T(8,128)S(1)}, f32[4,8,512]{2,1,0:T(8,128)S(1)}, u32[]{:S(2)}, u32[]{:S(2)}) collective-permute-start(f32[4,8,512]{2,1,0:T(8,128)S(1)} %pad_maximum_fusion.1.cols_ref), channel_id=1, source_target_pairs={{0,128},{8,136},{16,144},{24,152},{32,160},{40,168},{48,176},{56,1... | collective-permute-start | bytes 196616 | tf_op jit(solution)/shard_map/ppermute | solution.py:278
  38.1 1.8 %collective-permute-start.5 = (f32[16,48,128]{2,1,0:T(8,128)S(1)}, f32[16,48,128]{2,1,0:T(8,128)S(1)}, u32[]{:S(2)}, u32[]{:S(2)}) collective-permute-start(f32[16,48,128]{2,1,0:T(8,128)S(1)} %get-tuple-element.19), channel_id=1, source_target_pairs={{0,8},{8,0},{16,24},{24,16},{32,40},{40,32},{48,56},{56,48},{64,72... | collective-permute-start | bytes 1179656 | tf_op jit(solution)/shard_map/ppermute | solution.py:278
  40.7 19.3 %all-to-all-start = ((f32[16,48,128]{2,1,0:T(8,128)}), f32[16,48,128]{2,1,0:T(8,128)S(1)}, u32[]{:S(2)}, u32[]{:S(2)}) async-start(f32[16,48,128]{2,1,0:T(8,128)} %add.265), calls=%async_computation | async-start | bytes 786432 | tf_op jit(solution)/shard_map/all_to_all | solution.py:301
  45.0 19.1 %collective-permute-start.7 = (f32[2,8,128]{2,1,0:T(8,128)S(1)}, f32[2,8,128]{2,1,0:T(8,128)S(1)}, u32[]{:S(2)}, u32[]{:S(2)}) collective-permute-start(f32[2,8,128]{2,1,0:T(8,128)S(1)} %pad_maximum_fusion.6), channel_id=1, source_target_pairs={{0,1},{1,0},{2,3},{3,2},{4,5},{5,4},{6,7},{7,6},{8,9},{9,8},{10,11... | collective-permute-start | bytes 24584 | tf_op jit(solution)/shard_map/ppermute | solution.py:279
  60.7 13.3 %all-to-all-start.1 = ((f32[8,48,128]{2,1,0:T(8,128)}), f32[8,48,128]{2,1,0:T(8,128)S(1)}, u32[]{:S(2)}, u32[]{:S(2)}) async-start(f32[8,48,128]{2,1,0:T(8,128)} %broadcast_in_dim.21), calls=%async_computation.1 | async-start | bytes 393216 | tf_op jit(solution)/shard_map/all_to_all | solution.py:313
  64.1 5.3 %collective-permute-start.8 = (f32[4,8,128]{2,1,0:T(8,128)S(1)}, f32[4,8,128]{2,1,0:T(8,128)S(1)}, u32[]{:S(2)}, u32[]{:S(2)}) collective-permute-start(f32[4,8,128]{2,1,0:T(8,128)S(1)} %pad_maximum_fusion.4), channel_id=1, source_target_pairs={{0,2},{1,3},{2,0},{3,1},{4,6},{5,7},{6,4},{7,5},{8,10},{9,11},{10,... | collective-permute-start | bytes 49160 | tf_op jit(solution)/shard_map/ppermute | solution.py:279
  69.4 5.4 %collective-permute-start.9 = (f32[8,8,128]{2,1,0:T(8,128)S(1)}, f32[8,8,128]{2,1,0:T(8,128)S(1)}, u32[]{:S(2)}, u32[]{:S(2)}) collective-permute-start(f32[8,8,128]{2,1,0:T(8,128)S(1)} %pad_maximum_fusion.3), channel_id=1, source_target_pairs={{0,4},{1,5},{2,6},{3,7},{4,0},{5,1},{6,2},{7,3},{8,12},{9,13},{10,... | collective-permute-start | bytes 98312 | tf_op jit(solution)/shard_map/ppermute | solution.py:279
  74.0 12.9 %collective-permute-start.6 = (f32[8,48,128]{2,1,0:T(8,128)S(1)}, f32[8,48,128]{2,1,0:T(8,128)S(1)}, u32[]{:S(2)}, u32[]{:S(2)}) collective-permute-start(f32[8,48,128]{2,1,0:T(8,128)S(1)} %all-to-all-done.1.field_ref), channel_id=1, source_target_pairs={{0,8},{8,0},{16,24},{24,16},{32,40},{40,32},{48,56},{56,48},{64,72... | collective-permute-start | bytes 589832 | tf_op jit(solution)/shard_map/ppermute | solution.py:278
  120.4 1.4 %collective-permute-start.10 = (f32[8,48,128]{2,1,0:T(8,128)S(1)}, f32[8,48,128]{2,1,0:T(8,128)S(1)}, u32[]{:S(2)}, u32[]{:S(2)}) collective-permute-start(f32[8,48,128]{2,1,0:T(8,128)S(1)} %all_to_all.26.field_ref), channel_id=1, source_target_pairs={{0,8},{8,0},{16,24},{24,16},{32,40},{40,32},{48,56},{56,48},{64,72... | collective-permute-start | bytes 589832 | tf_op jit(solution)/shard_map/ppermute | solution.py:278

commit v4 on v3

--- a/solution.py
+++ b/solution.py
@@ -28,11 +28,6 @@
     rest = x - one
     two = rest.astype(jnp.bfloat16).astype(jnp.float32)
     return one, two, rest - two
-
-
-def padded(points):
-    fill = jnp.full((8 - points.shape[0], points.shape[1]), 0.5, jnp.float32)
-    return jnp.concatenate([points, fill], axis=0)
 
 
 def features(points, target, extra=None):
@@ -65,73 +60,68 @@
     return (square * square) * (5.0 - w)
 
 
-def stage_kernel(vol_ref, adj_ref, mask_ref, feat_ref, weights_ref, absent_ref, near_ref, held_ref, sem_ref):
-    copies = [
-        pltpu.make_async_copy(vol_ref, near_ref, sem_ref.at[0]),
-        pltpu.make_async_copy(mask_ref, held_ref, sem_ref.at[1]),
-        pltpu.make_async_copy(adj_ref, weights_ref, sem_ref.at[2]),
-    ]
-    for copy in copies:
-        copy.start()
-    for copy in copies:
-        copy.wait()
-    rows = vol_ref.shape[1]
-    tiles = rows // TILE
-    tile = lax.broadcasted_iota(jnp.int32, (tiles, rows), 0)
-    place = lax.broadcasted_iota(jnp.int32, (tiles, rows), 1) // TILE
-    onehot = jnp.where(tile == place, 1.0, 0.0)
-    feat_ref[...] = features(padded(near_ref[...]), False, onehot).T.astype(jnp.bfloat16)
-    absent_ref[...] = (1 - held_ref[...]).astype(jnp.float32)
-
-
-def stage(vol, adj, mask):
+def stage_kernel(own_ref, other_ref, mask_ref, mask_other_ref, feat_ref, weights_ref, absent_ref):
+    rows = own_ref.shape[1]
+    objs = weights_ref.shape[0]
+    tiles = mask_ref.shape[0]
+    for side, (held, held_mask) in enumerate(((own_ref, mask_ref), (other_ref, mask_other_ref))):
+        tile = lax.broadcasted_iota(jnp.int32, (2 * tiles, rows), 0)
+        place = lax.broadcasted_iota(jnp.int32, (2 * tiles, rows), 1) // TILE + side * tiles
+        onehot = jnp.where(tile == place, 1.0, 0.0)
+        source = features(held[objs:, :], False, onehot).T.astype(jnp.bfloat16)
+        feat_ref[side * rows:(side + 1) * rows, :] = source
+        weights_ref[:, side * rows:(side + 1) * rows] = held[:objs, :].astype(jnp.bfloat16)
+        absent_ref[side * tiles:(side + 1) * tiles, :] = 1.0 - held_mask[...]
+
+
+def stage(own, other, mask, mask_other):
+    objs = own.shape[0] - 8
+    rows = 2 * own.shape[1]
+    tiles = 2 * mask.shape[0]
     return pl.pallas_call(
         stage_kernel,
-        in_specs=[pl.BlockSpec(memory_space=pltpu.HBM)] * 3,
+        in_specs=[pl.BlockSpec(memory_space=pltpu.VMEM)] * 4,
         out_specs=[pl.BlockSpec(memory_space=pltpu.VMEM)] * 3,
         out_shape=(
-            jax.ShapeDtypeStruct((vol.shape[1], DEPTH), jnp.bfloat16),
-            jax.ShapeDtypeStruct(adj.shape, jnp.bfloat16),
-            jax.ShapeDtypeStruct(mask.shape, jnp.float32),
-        ),
-        scratch_shapes=[
-            pltpu.VMEM(vol.shape, jnp.float32),
-            pltpu.VMEM(mask.shape, jnp.int32),
-            pltpu.SemaphoreType.DMA((3,)),
-        ],
+            jax.ShapeDtypeStruct((rows, DEPTH), jnp.bfloat16),
+            jax.ShapeDtypeStruct((objs, rows), jnp.bfloat16),
+            jax.ShapeDtypeStruct((tiles, mask.shape[1]), jnp.float32),
+        ),
         name="stage",
         compiler_params=pltpu.CompilerParams(vmem_limit_bytes=GRANT),
         cost_estimate=pl.CostEstimate(flops=1 << 20, bytes_accessed=2 << 20, transcendentals=0),
-    )(*[pltpu.with_memory_space_constraint(x, pltpu.HBM) for x in (vol, adj, mask)])
+    )(own, other, mask, mask_other)
 
 
 def coupling_kernel(base, spot_ref, feat_ref, adj_ref, absent_ref, cols_ref, *refs):
+    out_ref = refs[-1]
     rows = feat_ref.shape[0]
-    width = cols_ref.shape[2]
-    far = (base + pl.program_id(0)) ^ spot_ref[1]
+    width = 2 * TILE
+    slot = base + 2 * pl.program_id(0)
     lower = (spot_ref[0] >> 1) & 1
 
-    tile = lax.broadcasted_iota(jnp.int32, (absent_ref.shape[1], width), 0)
-    piece = lax.broadcasted_iota(jnp.int32, (absent_ref.shape[1], width), 1) // TILE
-    swapped = (piece % 2) * 2 + piece // 2
-    pick = jnp.where(tile == 4 * far + (swapped ^ spot_ref[0]), 1.0, 0.0).astype(jnp.bfloat16)
+    tile = lax.broadcasted_iota(jnp.int32, (absent_ref.shape[1], 2 * width), 0)
+    piece = lax.broadcasted_iota(jnp.int32, (absent_ref.shape[1], 2 * width), 1) // TILE
+    owner = 4 * ((slot + piece // 2) ^ spot_ref[1]) + ((2 * (piece % 2)) ^ spot_ref[0])
+    pick = jnp.where(tile == owner, 1.0, 0.0).astype(jnp.bfloat16)
     barred = FAR * jnp.dot(absent_ref[...].astype(jnp.bfloat16), pick, preferred_element_type=jnp.float32)
-    target = features(cols_ref[0], True, barred).astype(jnp.bfloat16)
-
-    half = width // 2
+    points = jnp.concatenate([cols_ref[k, :, :width] for k in range(2)], axis=1)
+    target = features(points, True, barred).astype(jnp.bfloat16)
+
     step = 512
-    for side, out_ref in enumerate(refs[-2:]):
-        total = jnp.zeros((adj_ref.shape[0], half), jnp.float32)
+    for k in range(2):
+        total = jnp.zeros((adj_ref.shape[0], width), jnp.float32)
         for start in range(0, rows, step):
             d2 = jnp.dot(
                 feat_ref[start:start + step, :],
-                target[:, side * half:(side + 1) * half],
+                target[:, k * width:(k + 1) * width],
                 preferred_element_type=jnp.float32,
             )
             values = profile(d2).astype(jnp.bfloat16)
             total += jnp.dot(adj_ref[:, start:start + step], values, preferred_element_type=jnp.float32)
-        out_ref[lower] = total[:, :TILE]
-        out_ref[1 - lower] = total[:, TILE:]
+        place = 2 * (k ^ (spot_ref[1] & 1))
+        out_ref[place + lower] = total[:, :TILE]
+        out_ref[place + 1 - lower] = total[:, TILE:]
 
 
 def coupling(base, blocks, spot, staged, cols, earlier=()):
@@ -139,26 +129,24 @@
     count, axes, width = cols.shape
     objs = adj.shape[0]
     whole = lambda shape: pl.BlockSpec(shape, lambda i, s: (0,) * len(shape))
-    out = jax.ShapeDtypeStruct((2 * blocks, objs, TILE), jnp.float32)
-    place = pl.BlockSpec((2, objs, TILE), lambda i, s: ((base + i) ^ s[1], 0, 0))
     return pl.pallas_call(
         functools.partial(coupling_kernel, base),
         grid_spec=pltpu.PrefetchScalarGridSpec(
             num_scalar_prefetch=1,
-            grid=(count,),
+            grid=(count // 2,),
             in_specs=[
                 whole(feat.shape),
                 whole(adj.shape),
                 whole(absent.shape),
-                pl.BlockSpec((1, axes, width), lambda i, s: (i, 0, 0)),
+                pl.BlockSpec((2, axes, width), lambda i, s: (i, 0, 0)),
             ] + [pl.BlockSpec(memory_space=pl.ANY)] * len(earlier),
-            out_specs=[place] * 2,
-        ),
-        out_shape=(out, out),
+            out_specs=pl.BlockSpec((4, objs, TILE), lambda i, s: ((base // 2 + i) ^ (s[1] >> 1), 0, 0)),
+        ),
+        out_shape=jax.ShapeDtypeStruct((2 * blocks, objs, TILE), jnp.float32),
         input_output_aliases={5 + i: i for i in range(len(earlier))},
         compiler_params=pltpu.CompilerParams(vmem_limit_bytes=GRANT),
         cost_estimate=pl.CostEstimate(
-            flops=20 * feat.shape[0] * count * width, bytes_accessed=2 << 20, transcendentals=0
+            flops=40 * feat.shape[0] * count * TILE, bytes_accessed=2 << 20, transcendentals=0
         ),
     )(spot, feat, adj, absent, cols, *earlier)
 
@@ -178,8 +166,7 @@
     @pl.when(pl.program_id(1) == 0)
     def _():
         odd = spot_ref[1] & 1
-        pair = (points_ref[odd], points_ref[1 - odd])
-        pieces = [part[:, 2 * side * TILE:(2 * side + 1) * TILE] for side in range(2) for part in pair]
+        pieces = [points_ref[slot, :, at:at + TILE] for at in (0, 2 * TILE) for slot in (odd, 1 - odd)]
         source_ref[...] = features(jnp.concatenate(pieces, axis=1), False).T.astype(jnp.bfloat16)
 
     source = source_ref[...]
@@ -283,22 +270,26 @@
     wide = lax.axis_index("wide").astype(jnp.int32)
     spot = jnp.stack([wide & 3, wide >> 2, lax.axis_index("narrow").astype(jnp.int32)])
     own = jnp.pad(surf_points, ((0, 5), (0, 0)), constant_values=0.5)
-    staged = stage(vol_points, vol_adjoint, tile_mask)
     across = swap(own, 2)
-    pair = jnp.concatenate([own, across], axis=1)
+    beside = swap(own, 1)
+    trio = jnp.concatenate([own, across, beside], axis=1)[None]
     rows = jnp.stack([own, across])
-    quad = jnp.concatenate([pair, swap(pair, 1)], axis=1)[None]
+    fill = jnp.full((5, vol_points.shape[1]), 0.5, jnp.float32)
+    packed = join(join(vol_adjoint.astype(jnp.float32), vol_points), fill)
+    listed = tile_mask.astype(jnp.float32)
+    two = join(trio, swap(trio, 4))
+    packed_other = swap(packed, 1)
+    listed_other = swap(listed, 1)
+    four = join(two, swap(two, 8))
     rows = join(rows, side(rows, 1))
-    two = join(quad, swap(quad, 4))
+    staged = stage(packed, packed_other, listed, listed_other)
+    next_four = swap(four, 16)
     rows = join(rows, side(rows, 2))
-    four = join(two, swap(two, 8))
+    sums = coupling(0, far, spot, staged, four)
     rows = join(rows, side(rows, 4))
-    next_four = swap(four, 16)
-    sums = coupling(0, far, spot, staged, four)
-    keep, send = coupling(4, far, spot, staged, next_four, sums)
-    got = swap(send, 1)
+    sums = coupling(4, far, spot, staged, next_four, (sums,))
     block = gram(spot, join(four, next_four), rows)
-    parts = lax.all_to_all(keep + got, "wide", 0, 0, axis_index_groups=chips, tiled=True)
+    parts = lax.all_to_all(sums, "wide", 0, 0, axis_index_groups=chips, tiled=True)
 
     total_volume = vol_points.shape[1] * n_wide
     total_surface = surf_points.shape[1] * n_wide * n_narrow

time: 139 us -> 134 us (0.964)
  waiting for transfers between devices: 28 us -> 21.2 us
  other arithmetic: 1.62 us -> 3.32 us
    ppermute x8 -> x9, waiting for transfers between devices: 8.07 us -> 3.6 us  [body(): lax.ppermute(x, 'wide', [(i, i ^ bit) for i in range(n_wide)])]
    all_to_all x1, waiting for transfers between devices: 14.3 us -> 11.9 us  [body(): lax.all_to_all(sums, 'wide', 0, 0, axis_index_groups=chips, tiled=True)]
    convert_element_type x0 -> x2, other arithmetic: none -> 1.65 us  [the longest x1 0.95 us: body(): packed = join(join(vol_adjoint.astype(jnp.float32), vol_points), fill)]
    ppermute x8 -> x9, starting transfers between devices: 13.6 us -> 14 us  [body(): lax.ppermute(x, 'wide', [(i, i ^ bit) for i in range(n_wide)])]
  transfers between devices with their start and end apart: 13 -> 14, of which waited for: 10 -> 7; matrix products, arithmetic and copies ran while one was open for 1% -> 3% of each run, Pallas kernels for 16% -> 16%
where the time goes in v4:
time: 134 us; the launch traced here: 132 us
  blocking collectives  44.5 us (33%)
  Pallas kernels  33.1 us (25%)
  starting transfers between devices  27.3 us (20%)
  waiting for transfers between devices  21.2 us (16%)
  other arithmetic  3.32 us (2%)
  local copies, waits for them, and re-layouts  1.54 us (1%)
    all_to_all x2, blocking collectives, mixed(): lax.all_to_all(partial, ('narrow', 'wide'), 0, 0, axis_index_groups=plane...  28.1 us
    pallas_call x2, Pallas kernels, coupling(): pl.pallas_call(functools.partial(coupling_kernel, base), grid_spec=pltpu....  16.6 us
    all_to_all x1, blocking collectives, mixed(): lax.all_to_all(repeat(field, far), 'wide', 0, 0, axis_index_groups=column...  16.4 us
    ppermute x9, starting transfers between devices, body(): lax.ppermute(x, 'wide', [(i, i ^ bit) for i in range(n_wide)])  14 us
    all_to_all x1, waiting for transfers between devices, body(): lax.all_to_all(sums, 'wide', 0, 0, axis_index_groups=chips, tiled=True)  11.9 us
    pallas_call x1, Pallas kernels, gram(): pl.pallas_call(gram_kernel, grid_spec=pltpu.PrefetchScalarGridSpec(num_sc...  9.5 us
    pallas_call x4, Pallas kernels, mix(): pl.pallas_call(functools.partial(mix_kernel, fresh, side), in_specs=[vmem...  6.62 us
    ppermute x3, starting transfers between devices, body(): lax.ppermute(x, 'narrow', [(i, i ^ bit) for i in range(n_narrow)])  5.74 us
  transfers between devices with their start and end apart: 14, of which 7 were waited for; matrix products, arithmetic and copies ran while one was open for 3% of the time, Pallas kernels for 16%

profile of v4, /device:TPU:2, one launch (start us, length us, event | category | flops | bytes accessed | tf_op | source)
XLA Modules:
  0.0 131.8 jit_solution(7293200991304881560)
XLA Ops:
  0.6 0.0 copy-start
  0.6 0.8 pad_bitcast_fusion
  1.4 0.0 collective-permute-start.3
  1.4 1.6 %collective-permute-start.2 = (f32[8,128]{1,0:T(8,128)S(1)}, f32[8,128]{1,0:T(8,128)S(1)}, u32[]{:S(2)}, u32[]{:S(2)}) collective-permute-start(f32[8,128]{1,0:T(8,128)S(1)} %get-tuple-element.23), channel_id=1, source_target_pairs={{0,16},{8,24},{16,0},{24,8},{32,48},{40,56},{48,32},{56,40},{64,80... | collective-permute-start | bytes 12296 | tf_op jit(solution)/shard_map/ppermute | solution.py:265
  3.0 1.0 convert_element_type.6
  3.9 0.1 pad.28.clone
  4.0 0.9 maximum_maximum_fusion.own_ref
  4.9 0.3 collective-permute-start
  5.2 0.0 collective-permute-done.3
  5.2 0.0 collective-permute-done.2
  5.2 2.0 %collective-permute-start.4 = (f32[1,8,384]{2,1,0:T(8,128)S(1)}, f32[1,8,384]{2,1,0:T(8,128)S(1)}, u32[]{:S(2)}, u32[]{:S(2)}) collective-permute-start(f32[1,8,384]{2,1,0:T(8,128)S(1)} %maximum_bitcast_fusion), channel_id=1, source_target_pairs={{0,32},{8,40},{16,48},{24,56},{32,0},{40,8},{48,16},{56,24},{64,96... | collective-permute-start | bytes 36872 | tf_op jit(solution)/shard_map/ppermute | solution.py:265
  7.2 1.8 %collective-permute-done.4 = f32[1,8,384]{2,1,0:T(8,128)S(1)} collective-permute-done((f32[1,8,384]{2,1,0:T(8,128)S(1)}, f32[1,8,384]{2,1,0:T(8,128)S(1)}, u32[]{:S(2)}, u32[]{:S(2)}) %collective-permute-start.4) | collective-permute-done | bytes 12320 | tf_op jit(solution)/shard_map/ppermute | solution.py:265
  9.0 3.3 %collective-permute-start.5 = (f32[2,8,384]{2,1,0:T(8,128)S(1)}, f32[2,8,384]{2,1,0:T(8,128)S(1)}, u32[]{:S(2)}, u32[]{:S(2)}) collective-permute-start(f32[2,8,384]{2,1,0:T(8,128)S(1)} %pad_maximum_fusion.3), channel_id=1, source_target_pairs={{0,64},{8,72},{16,80},{24,88},{32,96},{40,104},{48,112},{56,120},{... | collective-permute-start | bytes 73736 | tf_op jit(solution)/shard_map/ppermute | solution.py:265
  12.3 0.7 convert_element_type.7.mask_ref
  13.0 0.0 collective-permute-start.1
  13.0 1.2 collective-permute-done.5
  14.1 6.8 %collective-permute-start.6 = (f32[4,8,384]{2,1,0:T(8,128)S(1)}, f32[4,8,384]{2,1,0:T(8,128)S(1)}, u32[]{:S(2)}, u32[]{:S(2)}) collective-permute-start(f32[4,8,384]{2,1,0:T(8,128)S(1)} %pad_maximum_fusion.1.cols_ref), channel_id=1, source_target_pairs={{0,128},{8,136},{16,144},{24,152},{32,160},{40,168},{48,176},{56,1... | collective-permute-start | bytes 147464 | tf_op jit(solution)/shard_map/ppermute | solution.py:265
  20.9 0.1 pad_add_fusion.spot_ref
  21.0 0.0 collective-permute-done.1.mask_other_ref
  21.0 0.0 collective-permute-done.other_ref
  21.0 0.4 stage.1
  21.4 8.3 %shard_map.59.refs_0_ = f32[16,48,128]{2,1,0:T(8,128)} custom-call(s32[3]{0:T(128)S(1)} %pad_add_fusion.spot_ref, bf16[4096,128]{1,0:T(8,128)(2,1)S(1)} %get-tuple-element.9.feat_ref, bf16[48,4096]{1,0:T(8,128)(2,1)S(1)} %get-tuple-element.10.adj_ref, f32[32,32]{1,0:T(8,128)S(1)} %get-tuple-element.11.absent_ref, f32[4,8,384]{2,1,0:T(8,128)S(1)} %pad_maximum_fusion.1.cols_ref), custom_call_target="tpu_custom_call" | custom-call | flops 83886080 | bytes 2097152 | tf_op jit(solution)/shard_map/pallas_call | solution.py:132
  29.7 0.0 collective-permute-done.6.cols_ref
  29.7 8.3 %shard_map.60 = f32[16,48,128]{2,1,0:T(8,128)} custom-call(s32[3]{0:T(128)S(1)} %pad_add_fusion.spot_ref, bf16[4096,128]{1,0:T(8,128)(2,1)S(1)} %get-tuple-element.9.feat_ref, bf16[48,4096]{1,0:T(8,128)(2,1)S(1)} %get-tuple-element.10.adj_ref, f32[32,32]{1,0:T(8,128)S(1)} %get-tuple-element.11.absent_ref, ...), custom_call_target="tpu_custom_call", output_to_operand_aliasing={{}: (5, {})} | custom-call | flops 83886080 | bytes 2097152 | tf_op jit(solution)/shard_map/pallas_call | solution.py:132
  38.0 4.1 %all-to-all-start = ((f32[16,48,128]{2,1,0:T(8,128)}), f32[16,48,128]{2,1,0:T(8,128)S(1)}, u32[]{:S(2)}, u32[]{:S(2)}) async-start(f32[16,48,128]{2,1,0:T(8,128)} %shard_map.60), calls=%async_computation | async-start | bytes 786432 | tf_op jit(solution)/shard_map/all_to_all | solution.py:292
  42.1 0.0 copy-done
  42.1 0.6 collective-permute-start.8
  42.7 11.9 %all-to-all-done = f32[16,48,128]{2,1,0:T(8,128)S(1)} async-done(((f32[16,48,128]{2,1,0:T(8,128)}), f32[16,48,128]{2,1,0:T(8,128)S(1)}, u32[]{:S(2)}, u32[]{:S(2)}) %all-to-all-start) | async-done | bytes 393248 | tf_op jit(solution)/shard_map/all_to_all | solution.py:292
  54.7 0.7 broadcast_in_dim.25
  55.4 3.6 %all-to-all-start.1 = ((f32[8,48,128]{2,1,0:T(8,128)}), f32[8,48,128]{2,1,0:T(8,128)S(1)}, u32[]{:S(2)}, u32[]{:S(2)}) async-start(f32[8,48,128]{2,1,0:T(8,128)} %broadcast_in_dim.25), calls=%async_computation.1 | async-start | bytes 393216 | tf_op jit(solution)/shard_map/all_to_all | solution.py:304
  59.0 0.0 collective-permute-done.8
  59.0 2.2 %collective-permute-start.9 = (f32[4,8,128]{2,1,0:T(8,128)S(1)}, f32[4,8,128]{2,1,0:T(8,128)S(1)}, u32[]{:S(2)}, u32[]{:S(2)}) collective-permute-start(f32[4,8,128]{2,1,0:T(8,128)S(1)} %pad_maximum_fusion.4), channel_id=1, source_target_pairs={{0,2},{1,3},{2,0},{3,1},{4,6},{5,7},{6,4},{7,5},{8,10},{9,11},{10,... | collective-permute-start | bytes 49160 | tf_op jit(solution)/shard_map/ppermute | solution.py:266
  61.2 3.1 %collective-permute-done.9 = f32[4,8,128]{2,1,0:T(8,128)S(1)} collective-permute-done((f32[4,8,128]{2,1,0:T(8,128)S(1)}, f32[4,8,128]{2,1,0:T(8,128)S(1)}, u32[]{:S(2)}, u32[]{:S(2)}) %collective-permute-start.9) | collective-permute-done | bytes 16416 | tf_op jit(solution)/shard_map/ppermute | solution.py:266
  64.3 2.9 %collective-permute-start.10 = (f32[8,8,128]{2,1,0:T(8,128)S(1)}, f32[8,8,128]{2,1,0:T(8,128)S(1)}, u32[]{:S(2)}, u32[]{:S(2)}) collective-permute-start(f32[8,8,128]{2,1,0:T(8,128)S(1)} %pad_maximum_fusion.2), channel_id=1, source_target_pairs={{0,4},{1,5},{2,6},{3,7},{4,0},{5,1},{6,2},{7,3},{8,12},{9,13},{10,... | collective-permute-start | bytes 98312 | tf_op jit(solution)/shard_map/ppermute | solution.py:266
  67.2 1.4 %all-to-all-done.1.field_ref = f32[8,48,128]{2,1,0:T(8,128)S(1)} async-done(((f32[8,48,128]{2,1,0:T(8,128)}), f32[8,48,128]{2,1,0:T(8,128)S(1)}, u32[]{:S(2)}, u32[]{:S(2)}) %all-to-all-start.1) | async-done | bytes 196640 | tf_op jit(solution)/shard_map/all_to_all | solution.py:304
  68.7 0.0 collective-permute-start.7
  68.7 1.1 collective-permute-done.10
  69.8 9.5 %gram.1.gram_ref = bf16[2,4,256,2048]{3,2,1,0:T(8,128)(2,1)} custom-call(s32[3]{0:T(128)S(1)} %pad_add_fusion.spot_ref, f32[8,8,384]{2,1,0:T(8,128)S(1)} %pad_maximum_fusion.points_ref, f32[16,8,128]{2,1,0:T(8,128)S(1)} %constant_dynamic-update-slice_fusion.rows_ref), custom_call_target="tpu_custom_call" | custom-call | flops 83886080 | bytes 8388608 | tf_op jit(solution)/shard_map/gram/pallas_call | solution.py:188
  79.3 2.5 %mix.4 = (f32[16,48,128]{2,1,0:T(8,128)S(1)}, bf16[4,256,2048]{2,1,0:T(8,128)(2,1)S(1)}) custom-call(f32[8,48,128]{2,1,0:T(8,128)S(1)} %all-to-all-done.1.field_ref, bf16[2,4,256,2048]{3,2,1,0:T(8,128)(2,1)} %gram.1.gram_ref), custom_call_target="tpu_custom_call" | custom-call | flops 402653184 | bytes 5242880 | tf_op jit(solution)/shard_map/mix/pallas_call | solution.py:243
  81.8 0.0 collective-permute-done.7.field_ref
  81.8 2.5 %mix.5 = (f32[16,48,128]{2,1,0:T(8,128)S(1)}, bf16[4,256,2048]{2,1,0:T(8,128)(2,1)S(1)}) custom-call(f32[8,48,128]{2,1,0:T(8,128)S(1)} %collective-permute-done.7.field_ref, bf16[2,4,256,2048]{3,2,1,0:T(8,128)(2,1)} %gram.1.gram_ref, f32[16,48,128]{2,1,0:T(8,128)S(1)} %get-tuple-element.12.refs_0_), custom_call_target="tpu_custom_call" | custom-call | flops 402653184 | bytes 5242880 | tf_op jit(solution)/shard_map/mix/pallas_call | solution.py:243
  84.3 14.5 %all_to_all.25 = f32[16,48,128]{2,1,0:T(8,128)S(1)} all-to-all(f32[16,48,128]{2,1,0:T(8,128)S(1)} %get-tuple-element.13), channel_id=1, replica_groups={{0,16,1,17,2,18,3,19,4,20,5,21,6,22,7,23},{8,24,9,25,10,26,11,27,12,28,..., dimensions={0} | all-to-all | bytes 786432 | tf_op jit(solution)/shard_map/all_to_all | solution.py:309
  98.9 16.4 %all_to_all.26.field_ref = f32[8,48,128]{2,1,0:T(8,128)S(1)} all-to-all(f32[8,48,128]{2,1,0:T(8,128)S(1)} %broadcast_in_dim.27), channel_id=1, replica_groups={{0,32,64,96,128,160,192,224},{8,40,72,104,136,168,200,232},{16,48,80,11..., dimensions={0} | all-to-all | bytes 393216 | tf_op jit(solution)/shard_map/all_to_all | solution.py:304
  115.3 0.0 collective-permute-start.11
  115.3 0.8 mix.6.refs_0_
  116.1 0.6 collective-permute-done.11.field_ref
  116.7 0.8 mix.7
  117.5 13.6 %all_to_all.27 = f32[16,48,128]{2,1,0:T(8,128)S(1)} all-to-all(f32[16,48,128]{2,1,0:T(8,128)S(1)} %mix.7), channel_id=1, replica_groups={{0,16,1,17,2,18,3,19,4,20,5,21,6,22,7,23},{8,24,9,25,10,26,11,27,12,28,..., dimensions={0} | all-to-all | bytes 786432 | tf_op jit(solution)/shard_map/all_to_all | solution.py:309
  131.2 0.6 fusion.3
  (16 shorter events, 0.1 us)
Async XLA Ops:
  0.6 41.5 %copy-start = (f32[3,128]{1,0:T(4,128)S(1)}, f32[3,128]{1,0:T(4,128)}, u32[]{:S(2)}) copy-start(f32[3,128]{1,0:T(4,128)} %param.6) | copy-start | bytes 4612
  1.4 3.8 %collective-permute-start.3 = (f32[8,128]{1,0:T(8,128)S(1)}, f32[8,128]{1,0:T(8,128)S(1)}, u32[]{:S(2)}, u32[]{:S(2)}) collective-permute-start(f32[8,128]{1,0:T(8,128)S(1)} %get-tuple-element.23), channel_id=1, source_target_pairs={{0,8},{8,0},{16,24},{24,16},{32,40},{40,32},{48,56},{56,48},{64,72... | collective-permute-start | bytes 12296 | tf_op jit(solution)/shard_map/ppermute | solution.py:265
  1.4 3.8 %collective-permute-start.2 = (f32[8,128]{1,0:T(8,128)S(1)}, f32[8,128]{1,0:T(8,128)S(1)}, u32[]{:S(2)}, u32[]{:S(2)}) collective-permute-start(f32[8,128]{1,0:T(8,128)S(1)} %get-tuple-element.23), channel_id=1, source_target_pairs={{0,16},{8,24},{16,0},{24,8},{32,48},{40,56},{48,32},{56,40},{64,80... | collective-permute-start | bytes 12296 | tf_op jit(solution)/shard_map/ppermute | solution.py:265
  4.9 16.1 %collective-permute-start = (f32[56,2048]{1,0:T(8,128)S(1)}, f32[56,2048]{1,0:T(8,128)S(1)}, u32[]{:S(2)}, u32[]{:S(2)}) collective-permute-start(f32[56,2048]{1,0:T(8,128)S(1)} %maximum_maximum_fusion.own_ref), channel_id=1, source_target_pairs={{0,8},{8,0},{16,24},{24,16},{32,40},{40,32},{48,56},{56,48},{64,72... | collective-permute-start | bytes 1376264 | tf_op jit(solution)/shard_map/ppermute | solution.py:265
  5.2 3.8 %collective-permute-start.4 = (f32[1,8,384]{2,1,0:T(8,128)S(1)}, f32[1,8,384]{2,1,0:T(8,128)S(1)}, u32[]{:S(2)}, u32[]{:S(2)}) collective-permute-start(f32[1,8,384]{2,1,0:T(8,128)S(1)} %maximum_bitcast_fusion), channel_id=1, source_target_pairs={{0,32},{8,40},{16,48},{24,56},{32,0},{40,8},{48,16},{56,24},{64,96... | collective-permute-start | bytes 36872 | tf_op jit(solution)/shard_map/ppermute | solution.py:265
  9.0 5.1 %collective-permute-start.5 = (f32[2,8,384]{2,1,0:T(8,128)S(1)}, f32[2,8,384]{2,1,0:T(8,128)S(1)}, u32[]{:S(2)}, u32[]{:S(2)}) collective-permute-start(f32[2,8,384]{2,1,0:T(8,128)S(1)} %pad_maximum_fusion.3), channel_id=1, source_target_pairs={{0,64},{8,72},{16,80},{24,88},{32,96},{40,104},{48,112},{56,120},{... | collective-permute-start | bytes 73736 | tf_op jit(solution)/shard_map/ppermute | solution.py:265
  13.0 8.0 %collective-permute-start.1 = (f32[16,32]{1,0:T(8,128)S(1)}, f32[16,32]{1,0:T(8,128)S(1)}, u32[]{:S(2)}, u32[]{:S(2)}) collective-permute-start(f32[16,32]{1,0:T(8,128)S(1)} %convert_element_type.7.mask_ref), channel_id=1, source_target_pairs={{0,8},{8,0},{16,24},{24,16},{32,40},{40,32},{48,56},{56,48},{64,72... | collective-permute-start | bytes 6152 | tf_op jit(solution)/shard_map/ppermute | solution.py:265
  14.1 15.6 %collective-permute-start.6 = (f32[4,8,384]{2,1,0:T(8,128)S(1)}, f32[4,8,384]{2,1,0:T(8,128)S(1)}, u32[]{:S(2)}, u32[]{:S(2)}) collective-permute-start(f32[4,8,384]{2,1,0:T(8,128)S(1)} %pad_maximum_fusion.1.cols_ref), channel_id=1, source_target_pairs={{0,128},{8,136},{16,144},{24,152},{32,160},{40,168},{48,176},{56,1... | collective-permute-start | bytes 147464 | tf_op jit(solution)/shard_map/ppermute | solution.py:265
  38.0 16.7 %all-to-all-start = ((f32[16,48,128]{2,1,0:T(8,128)}), f32[16,48,128]{2,1,0:T(8,128)S(1)}, u32[]{:S(2)}, u32[]{:S(2)}) async-start(f32[16,48,128]{2,1,0:T(8,128)} %shard_map.60), calls=%async_computation | async-start | bytes 786432 | tf_op jit(solution)/shard_map/all_to_all | solution.py:292
  42.1 16.9 %collective-permute-start.8 = (f32[2,8,128]{2,1,0:T(8,128)S(1)}, f32[2,8,128]{2,1,0:T(8,128)S(1)}, u32[]{:S(2)}, u32[]{:S(2)}) collective-permute-start(f32[2,8,128]{2,1,0:T(8,128)S(1)} %pad_maximum_fusion.5), channel_id=1, source_target_pairs={{0,1},{1,0},{2,3},{3,2},{4,5},{5,4},{6,7},{7,6},{8,9},{9,8},{10,11... | collective-permute-start | bytes 24584 | tf_op jit(solution)/shard_map/ppermute | solution.py:266
  55.4 13.3 %all-to-all-start.1 = ((f32[8,48,128]{2,1,0:T(8,128)}), f32[8,48,128]{2,1,0:T(8,128)S(1)}, u32[]{:S(2)}, u32[]{:S(2)}) async-start(f32[8,48,128]{2,1,0:T(8,128)} %broadcast_in_dim.25), calls=%async_computation.1 | async-start | bytes 393216 | tf_op jit(solution)/shard_map/all_to_all | solution.py:304
  59.0 5.3 %collective-permute-start.9 = (f32[4,8,128]{2,1,0:T(8,128)S(1)}, f32[4,8,128]{2,1,0:T(8,128)S(1)}, u32[]{:S(2)}, u32[]{:S(2)}) collective-permute-start(f32[4,8,128]{2,1,0:T(8,128)S(1)} %pad_maximum_fusion.4), channel_id=1, source_target_pairs={{0,2},{1,3},{2,0},{3,1},{4,6},{5,7},{6,4},{7,5},{8,10},{9,11},{10,... | collective-permute-start | bytes 49160 | tf_op jit(solution)/shard_map/ppermute | solution.py:266
  64.3 5.4 %collective-permute-start.10 = (f32[8,8,128]{2,1,0:T(8,128)S(1)}, f32[8,8,128]{2,1,0:T(8,128)S(1)}, u32[]{:S(2)}, u32[]{:S(2)}) collective-permute-start(f32[8,8,128]{2,1,0:T(8,128)S(1)} %pad_maximum_fusion.2), channel_id=1, source_target_pairs={{0,4},{1,5},{2,6},{3,7},{4,0},{5,1},{6,2},{7,3},{8,12},{9,13},{10,... | collective-permute-start | bytes 98312 | tf_op jit(solution)/shard_map/ppermute | solution.py:266
  68.7 13.1 %collective-permute-start.7 = (f32[8,48,128]{2,1,0:T(8,128)S(1)}, f32[8,48,128]{2,1,0:T(8,128)S(1)}, u32[]{:S(2)}, u32[]{:S(2)}) collective-permute-start(f32[8,48,128]{2,1,0:T(8,128)S(1)} %all-to-all-done.1.field_ref), channel_id=1, source_target_pairs={{0,8},{8,0},{16,24},{24,16},{32,40},{40,32},{48,56},{56,48},{64,72... | collective-permute-start | bytes 589832 | tf_op jit(solution)/shard_map/ppermute | solution.py:265
  115.3 1.4 %collective-permute-start.11 = (f32[8,48,128]{2,1,0:T(8,128)S(1)}, f32[8,48,128]{2,1,0:T(8,128)S(1)}, u32[]{:S(2)}, u32[]{:S(2)}) collective-permute-start(f32[8,48,128]{2,1,0:T(8,128)S(1)} %all_to_all.26.field_ref), channel_id=1, source_target_pairs={{0,8},{8,0},{16,24},{24,16},{32,40},{40,32},{48,56},{56,48},{64,72... | collective-permute-start | bytes 589832 | tf_op jit(solution)/shard_map/ppermute | solution.py:265

commit v5 on v4

--- a/solution.py
+++ b/solution.py
@@ -97,19 +97,20 @@
     out_ref = refs[-1]
     rows = feat_ref.shape[0]
     width = 2 * TILE
-    slot = base + 2 * pl.program_id(0)
+    group = cols_ref.shape[0]
+    slot = base + group * pl.program_id(0)
     lower = (spot_ref[0] >> 1) & 1
 
-    tile = lax.broadcasted_iota(jnp.int32, (absent_ref.shape[1], 2 * width), 0)
-    piece = lax.broadcasted_iota(jnp.int32, (absent_ref.shape[1], 2 * width), 1) // TILE
+    tile = lax.broadcasted_iota(jnp.int32, (absent_ref.shape[1], group * width), 0)
+    piece = lax.broadcasted_iota(jnp.int32, (absent_ref.shape[1], group * width), 1) // TILE
     owner = 4 * ((slot + piece // 2) ^ spot_ref[1]) + ((2 * (piece % 2)) ^ spot_ref[0])
     pick = jnp.where(tile == owner, 1.0, 0.0).astype(jnp.bfloat16)
     barred = FAR * jnp.dot(absent_ref[...].astype(jnp.bfloat16), pick, preferred_element_type=jnp.float32)
-    points = jnp.concatenate([cols_ref[k, :, :width] for k in range(2)], axis=1)
+    points = jnp.concatenate([cols_ref[k, :, :width] for k in range(group)], axis=1)
     target = features(points, True, barred).astype(jnp.bfloat16)
 
     step = 512
-    for k in range(2):
+    for k in range(group):
         total = jnp.zeros((adj_ref.shape[0], width), jnp.float32)
         for start in range(0, rows, step):
             d2 = jnp.dot(
@@ -119,7 +120,7 @@
             )
             values = profile(d2).astype(jnp.bfloat16)
             total += jnp.dot(adj_ref[:, start:start + step], values, preferred_element_type=jnp.float32)
-        place = 2 * (k ^ (spot_ref[1] & 1))
+        place = 2 * (k ^ (spot_ref[1] & (group - 1)))
         out_ref[place + lower] = total[:, :TILE]
         out_ref[place + 1 - lower] = total[:, TILE:]
 
@@ -128,19 +129,20 @@
     feat, adj, absent = staged
     count, axes, width = cols.shape
     objs = adj.shape[0]
+    group = 4
     whole = lambda shape: pl.BlockSpec(shape, lambda i, s: (0,) * len(shape))
     return pl.pallas_call(
         functools.partial(coupling_kernel, base),
         grid_spec=pltpu.PrefetchScalarGridSpec(
             num_scalar_prefetch=1,
-            grid=(count // 2,),
+            grid=(count // group,),
             in_specs=[
                 whole(feat.shape),
                 whole(adj.shape),
                 whole(absent.shape),
-                pl.BlockSpec((2, axes, width), lambda i, s: (i, 0, 0)),
+                pl.BlockSpec((group, axes, width), lambda i, s: (i, 0, 0)),
             ] + [pl.BlockSpec(memory_space=pl.ANY)] * len(earlier),
-            out_specs=pl.BlockSpec((4, objs, TILE), lambda i, s: ((base // 2 + i) ^ (s[1] >> 1), 0, 0)),
+            out_specs=pl.BlockSpec((2 * group, objs, TILE), lambda i, s: ((base // group + i) ^ (s[1] // group), 0, 0)),
         ),
         out_shape=jax.ShapeDtypeStruct((2 * blocks, objs, TILE), jnp.float32),
         input_output_aliases={5 + i: i for i in range(len(earlier))},

time: 134 us -> 133 us (level)
  no operation moved by 1% of the time
where the time goes in v5:
time: 133 us; the launch traced here: 131 us
  blocking collectives  44.5 us (33%)
  Pallas kernels  32.7 us (25%)
  starting transfers between devices  27.1 us (20%)
  waiting for transfers between devices  21.4 us (16%)
  other arithmetic  3.32 us (2%)
  local copies, waits for them, and re-layouts  1.54 us (1%)
    all_to_all x2, blocking collectives, mixed(): lax.all_to_all(partial, ('narrow', 'wide'), 0, 0, axis_index_groups=plane...  28.1 us
    all_to_all x1, blocking collectives, mixed(): lax.all_to_all(repeat(field, far), 'wide', 0, 0, axis_index_groups=column...  16.4 us
    pallas_call x2, Pallas kernels, coupling(): pl.pallas_call(functools.partial(coupling_kernel, base), grid_spec=pltpu....  16.2 us
    ppermute x9, starting transfers between devices, body(): lax.ppermute(x, 'wide', [(i, i ^ bit) for i in range(n_wide)])  14 us
    all_to_all x1, waiting for transfers between devices, body(): lax.all_to_all(sums, 'wide', 0, 0, axis_index_groups=chips, tiled=True)  12.1 us
    pallas_call x1, Pallas kernels, gram(): pl.pallas_call(gram_kernel, grid_spec=pltpu.PrefetchScalarGridSpec(num_sc...  9.5 us
    pallas_call x4, Pallas kernels, mix(): pl.pallas_call(functools.partial(mix_kernel, fresh, side), in_specs=[vmem...  6.62 us
    ppermute x3, starting transfers between devices, body(): lax.ppermute(x, 'narrow', [(i, i ^ bit) for i in range(n_narrow)])  5.72 us
  transfers between devices with their start and end apart: 14, of which 7 were waited for; matrix products, arithmetic and copies ran while one was open for 3% of the time, Pallas kernels for 16%

profile of v5, /device:TPU:2, one launch (start us, length us, event | category | flops | bytes accessed | tf_op | source)
XLA Modules:
  0.0 131.4 jit_solution(270935102640377781)
XLA Ops:
  0.6 0.0 copy-start
  0.6 0.8 pad_bitcast_fusion
  1.4 0.0 collective-permute-start.3
  1.4 1.6 %collective-permute-start.2 = (f32[8,128]{1,0:T(8,128)S(1)}, f32[8,128]{1,0:T(8,128)S(1)}, u32[]{:S(2)}, u32[]{:S(2)}) collective-permute-start(f32[8,128]{1,0:T(8,128)S(1)} %get-tuple-element.23), channel_id=1, source_target_pairs={{0,16},{8,24},{16,0},{24,8},{32,48},{40,56},{48,32},{56,40},{64,80... | collective-permute-start | bytes 12296 | tf_op jit(solution)/shard_map/ppermute | solution.py:267
  3.0 1.0 convert_element_type.6
  3.9 0.1 pad.28.clone
  4.0 0.9 maximum_maximum_fusion.own_ref
  4.9 0.3 collective-permute-start
  5.2 0.0 collective-permute-done.3
  5.2 0.0 collective-permute-done.2
  5.2 2.0 %collective-permute-start.4 = (f32[1,8,384]{2,1,0:T(8,128)S(1)}, f32[1,8,384]{2,1,0:T(8,128)S(1)}, u32[]{:S(2)}, u32[]{:S(2)}) collective-permute-start(f32[1,8,384]{2,1,0:T(8,128)S(1)} %maximum_bitcast_fusion), channel_id=1, source_target_pairs={{0,32},{8,40},{16,48},{24,56},{32,0},{40,8},{48,16},{56,24},{64,96... | collective-permute-start | bytes 36872 | tf_op jit(solution)/shard_map/ppermute | solution.py:267
  7.2 1.8 %collective-permute-done.4 = f32[1,8,384]{2,1,0:T(8,128)S(1)} collective-permute-done((f32[1,8,384]{2,1,0:T(8,128)S(1)}, f32[1,8,384]{2,1,0:T(8,128)S(1)}, u32[]{:S(2)}, u32[]{:S(2)}) %collective-permute-start.4) | collective-permute-done | bytes 12320 | tf_op jit(solution)/shard_map/ppermute | solution.py:267
  9.0 3.3 %collective-permute-start.5 = (f32[2,8,384]{2,1,0:T(8,128)S(1)}, f32[2,8,384]{2,1,0:T(8,128)S(1)}, u32[]{:S(2)}, u32[]{:S(2)}) collective-permute-start(f32[2,8,384]{2,1,0:T(8,128)S(1)} %pad_maximum_fusion.3), channel_id=1, source_target_pairs={{0,64},{8,72},{16,80},{24,88},{32,96},{40,104},{48,112},{56,120},{... | collective-permute-start | bytes 73736 | tf_op jit(solution)/shard_map/ppermute | solution.py:267
  12.3 0.7 convert_element_type.7.mask_ref
  13.0 0.0 collective-permute-start.1
  13.0 1.2 collective-permute-done.5
  14.1 6.8 %collective-permute-start.6 = (f32[4,8,384]{2,1,0:T(8,128)S(1)}, f32[4,8,384]{2,1,0:T(8,128)S(1)}, u32[]{:S(2)}, u32[]{:S(2)}) collective-permute-start(f32[4,8,384]{2,1,0:T(8,128)S(1)} %pad_maximum_fusion.1.cols_ref), channel_id=1, source_target_pairs={{0,128},{8,136},{16,144},{24,152},{32,160},{40,168},{48,176},{56,1... | collective-permute-start | bytes 147464 | tf_op jit(solution)/shard_map/ppermute | solution.py:267
  20.9 0.1 pad_add_fusion.spot_ref
  21.0 0.0 collective-permute-done.1.mask_other_ref
  21.0 0.0 collective-permute-done.other_ref
  21.0 0.4 stage.1
  21.4 8.0 %shard_map.59.refs_0_ = f32[16,48,128]{2,1,0:T(8,128)} custom-call(s32[3]{0:T(128)S(1)} %pad_add_fusion.spot_ref, bf16[4096,128]{1,0:T(8,128)(2,1)S(1)} %get-tuple-element.9.feat_ref, bf16[48,4096]{1,0:T(8,128)(2,1)S(1)} %get-tuple-element.10.adj_ref, f32[32,32]{1,0:T(8,128)S(1)} %get-tuple-element.11.absent_ref, f32[4,8,384]{2,1,0:T(8,128)S(1)} %pad_maximum_fusion.1.cols_ref), custom_call_target="tpu_custom_call" | custom-call | flops 83886080 | bytes 2097152 | tf_op jit(solution)/shard_map/pallas_call | solution.py:134
  29.4 0.0 collective-permute-done.6.cols_ref
  29.4 8.2 %shard_map.60 = f32[16,48,128]{2,1,0:T(8,128)} custom-call(s32[3]{0:T(128)S(1)} %pad_add_fusion.spot_ref, bf16[4096,128]{1,0:T(8,128)(2,1)S(1)} %get-tuple-element.9.feat_ref, bf16[48,4096]{1,0:T(8,128)(2,1)S(1)} %get-tuple-element.10.adj_ref, f32[32,32]{1,0:T(8,128)S(1)} %get-tuple-element.11.absent_ref, ...), custom_call_target="tpu_custom_call", output_to_operand_aliasing={{}: (5, {})} | custom-call | flops 83886080 | bytes 2097152 | tf_op jit(solution)/shard_map/pallas_call | solution.py:134
  37.6 4.0 %all-to-all-start = ((f32[16,48,128]{2,1,0:T(8,128)}), f32[16,48,128]{2,1,0:T(8,128)S(1)}, u32[]{:S(2)}, u32[]{:S(2)}) async-start(f32[16,48,128]{2,1,0:T(8,128)} %shard_map.60), calls=%async_computation | async-start | bytes 786432 | tf_op jit(solution)/shard_map/all_to_all | solution.py:294
  41.6 0.0 copy-done
  41.7 0.6 collective-permute-start.8
  42.3 12.1 %all-to-all-done = f32[16,48,128]{2,1,0:T(8,128)S(1)} async-done(((f32[16,48,128]{2,1,0:T(8,128)}), f32[16,48,128]{2,1,0:T(8,128)S(1)}, u32[]{:S(2)}, u32[]{:S(2)}) %all-to-all-start) | async-done | bytes 393248 | tf_op jit(solution)/shard_map/all_to_all | solution.py:294
  54.5 0.7 broadcast_in_dim.25
  55.1 3.4 %all-to-all-start.1 = ((f32[8,48,128]{2,1,0:T(8,128)}), f32[8,48,128]{2,1,0:T(8,128)S(1)}, u32[]{:S(2)}, u32[]{:S(2)}) async-start(f32[8,48,128]{2,1,0:T(8,128)} %broadcast_in_dim.25), calls=%async_computation.1 | async-start | bytes 393216 | tf_op jit(solution)/shard_map/all_to_all | solution.py:306
  58.5 0.0 collective-permute-done.8
  58.6 2.2 %collective-permute-start.9 = (f32[4,8,128]{2,1,0:T(8,128)S(1)}, f32[4,8,128]{2,1,0:T(8,128)S(1)}, u32[]{:S(2)}, u32[]{:S(2)}) collective-permute-start(f32[4,8,128]{2,1,0:T(8,128)S(1)} %pad_maximum_fusion.4), channel_id=1, source_target_pairs={{0,2},{1,3},{2,0},{3,1},{4,6},{5,7},{6,4},{7,5},{8,10},{9,11},{10,... | collective-permute-start | bytes 49160 | tf_op jit(solution)/shard_map/ppermute | solution.py:268
  60.8 3.1 %collective-permute-done.9 = f32[4,8,128]{2,1,0:T(8,128)S(1)} collective-permute-done((f32[4,8,128]{2,1,0:T(8,128)S(1)}, f32[4,8,128]{2,1,0:T(8,128)S(1)}, u32[]{:S(2)}, u32[]{:S(2)}) %collective-permute-start.9) | collective-permute-done | bytes 16416 | tf_op jit(solution)/shard_map/ppermute | solution.py:268
  63.9 2.9 %collective-permute-start.10 = (f32[8,8,128]{2,1,0:T(8,128)S(1)}, f32[8,8,128]{2,1,0:T(8,128)S(1)}, u32[]{:S(2)}, u32[]{:S(2)}) collective-permute-start(f32[8,8,128]{2,1,0:T(8,128)S(1)} %pad_maximum_fusion.2), channel_id=1, source_target_pairs={{0,4},{1,5},{2,6},{3,7},{4,0},{5,1},{6,2},{7,3},{8,12},{9,13},{10,... | collective-permute-start | bytes 98312 | tf_op jit(solution)/shard_map/ppermute | solution.py:268
  66.8 1.4 %all-to-all-done.1.field_ref = f32[8,48,128]{2,1,0:T(8,128)S(1)} async-done(((f32[8,48,128]{2,1,0:T(8,128)}), f32[8,48,128]{2,1,0:T(8,128)S(1)}, u32[]{:S(2)}, u32[]{:S(2)}) %all-to-all-start.1) | async-done | bytes 196640 | tf_op jit(solution)/shard_map/all_to_all | solution.py:306
  68.2 0.0 collective-permute-start.7
  68.2 1.1 collective-permute-done.10
  69.3 9.5 %gram.1.gram_ref = bf16[2,4,256,2048]{3,2,1,0:T(8,128)(2,1)} custom-call(s32[3]{0:T(128)S(1)} %pad_add_fusion.spot_ref, f32[8,8,384]{2,1,0:T(8,128)S(1)} %pad_maximum_fusion.points_ref, f32[16,8,128]{2,1,0:T(8,128)S(1)} %constant_dynamic-update-slice_fusion.rows_ref), custom_call_target="tpu_custom_call" | custom-call | flops 83886080 | bytes 8388608 | tf_op jit(solution)/shard_map/gram/pallas_call | solution.py:190
  78.8 2.5 %mix.4 = (f32[16,48,128]{2,1,0:T(8,128)S(1)}, bf16[4,256,2048]{2,1,0:T(8,128)(2,1)S(1)}) custom-call(f32[8,48,128]{2,1,0:T(8,128)S(1)} %all-to-all-done.1.field_ref, bf16[2,4,256,2048]{3,2,1,0:T(8,128)(2,1)} %gram.1.gram_ref), custom_call_target="tpu_custom_call" | custom-call | flops 402653184 | bytes 5242880 | tf_op jit(solution)/shard_map/mix/pallas_call | solution.py:245
  81.4 0.0 collective-permute-done.7.field_ref
  81.4 2.5 %mix.5 = (f32[16,48,128]{2,1,0:T(8,128)S(1)}, bf16[4,256,2048]{2,1,0:T(8,128)(2,1)S(1)}) custom-call(f32[8,48,128]{2,1,0:T(8,128)S(1)} %collective-permute-done.7.field_ref, bf16[2,4,256,2048]{3,2,1,0:T(8,128)(2,1)} %gram.1.gram_ref, f32[16,48,128]{2,1,0:T(8,128)S(1)} %get-tuple-element.12.refs_0_), custom_call_target="tpu_custom_call" | custom-call | flops 402653184 | bytes 5242880 | tf_op jit(solution)/shard_map/mix/pallas_call | solution.py:245
  83.9 14.5 %all_to_all.25 = f32[16,48,128]{2,1,0:T(8,128)S(1)} all-to-all(f32[16,48,128]{2,1,0:T(8,128)S(1)} %get-tuple-element.13), channel_id=1, replica_groups={{0,16,1,17,2,18,3,19,4,20,5,21,6,22,7,23},{8,24,9,25,10,26,11,27,12,28,..., dimensions={0} | all-to-all | bytes 786432 | tf_op jit(solution)/shard_map/all_to_all | solution.py:311
  98.4 16.4 %all_to_all.26.field_ref = f32[8,48,128]{2,1,0:T(8,128)S(1)} all-to-all(f32[8,48,128]{2,1,0:T(8,128)S(1)} %broadcast_in_dim.27), channel_id=1, replica_groups={{0,32,64,96,128,160,192,224},{8,40,72,104,136,168,200,232},{16,48,80,11..., dimensions={0} | all-to-all | bytes 393216 | tf_op jit(solution)/shard_map/all_to_all | solution.py:306
  114.8 0.0 collective-permute-start.11
  114.8 0.8 mix.6.refs_0_
  115.6 0.6 collective-permute-done.11.field_ref
  116.3 0.8 mix.7
  117.1 13.6 %all_to_all.27 = f32[16,48,128]{2,1,0:T(8,128)S(1)} all-to-all(f32[16,48,128]{2,1,0:T(8,128)S(1)} %mix.7), channel_id=1, replica_groups={{0,16,1,17,2,18,3,19,4,20,5,21,6,22,7,23},{8,24,9,25,10,26,11,27,12,28,..., dimensions={0} | all-to-all | bytes 786432 | tf_op jit(solution)/shard_map/all_to_all | solution.py:311
  130.7 0.6 fusion.3
  (16 shorter events, 0.1 us)
Async XLA Ops:
  0.6 41.0 %copy-start = (f32[3,128]{1,0:T(4,128)S(1)}, f32[3,128]{1,0:T(4,128)}, u32[]{:S(2)}) copy-start(f32[3,128]{1,0:T(4,128)} %param.6) | copy-start | bytes 4612
  1.4 3.8 %collective-permute-start.3 = (f32[8,128]{1,0:T(8,128)S(1)}, f32[8,128]{1,0:T(8,128)S(1)}, u32[]{:S(2)}, u32[]{:S(2)}) collective-permute-start(f32[8,128]{1,0:T(8,128)S(1)} %get-tuple-element.23), channel_id=1, source_target_pairs={{0,8},{8,0},{16,24},{24,16},{32,40},{40,32},{48,56},{56,48},{64,72... | collective-permute-start | bytes 12296 | tf_op jit(solution)/shard_map/ppermute | solution.py:267
  1.4 3.8 %collective-permute-start.2 = (f32[8,128]{1,0:T(8,128)S(1)}, f32[8,128]{1,0:T(8,128)S(1)}, u32[]{:S(2)}, u32[]{:S(2)}) collective-permute-start(f32[8,128]{1,0:T(8,128)S(1)} %get-tuple-element.23), channel_id=1, source_target_pairs={{0,16},{8,24},{16,0},{24,8},{32,48},{40,56},{48,32},{56,40},{64,80... | collective-permute-start | bytes 12296 | tf_op jit(solution)/shard_map/ppermute | solution.py:267
  4.9 16.1 %collective-permute-start = (f32[56,2048]{1,0:T(8,128)S(1)}, f32[56,2048]{1,0:T(8,128)S(1)}, u32[]{:S(2)}, u32[]{:S(2)}) collective-permute-start(f32[56,2048]{1,0:T(8,128)S(1)} %maximum_maximum_fusion.own_ref), channel_id=1, source_target_pairs={{0,8},{8,0},{16,24},{24,16},{32,40},{40,32},{48,56},{56,48},{64,72... | collective-permute-start | bytes 1376264 | tf_op jit(solution)/shard_map/ppermute | solution.py:267
  5.2 3.8 %collective-permute-start.4 = (f32[1,8,384]{2,1,0:T(8,128)S(1)}, f32[1,8,384]{2,1,0:T(8,128)S(1)}, u32[]{:S(2)}, u32[]{:S(2)}) collective-permute-start(f32[1,8,384]{2,1,0:T(8,128)S(1)} %maximum_bitcast_fusion), channel_id=1, source_target_pairs={{0,32},{8,40},{16,48},{24,56},{32,0},{40,8},{48,16},{56,24},{64,96... | collective-permute-start | bytes 36872 | tf_op jit(solution)/shard_map/ppermute | solution.py:267
  9.0 5.1 %collective-permute-start.5 = (f32[2,8,384]{2,1,0:T(8,128)S(1)}, f32[2,8,384]{2,1,0:T(8,128)S(1)}, u32[]{:S(2)}, u32[]{:S(2)}) collective-permute-start(f32[2,8,384]{2,1,0:T(8,128)S(1)} %pad_maximum_fusion.3), channel_id=1, source_target_pairs={{0,64},{8,72},{16,80},{24,88},{32,96},{40,104},{48,112},{56,120},{... | collective-permute-start | bytes 73736 | tf_op jit(solution)/shard_map/ppermute | solution.py:267
  13.0 8.0 %collective-permute-start.1 = (f32[16,32]{1,0:T(8,128)S(1)}, f32[16,32]{1,0:T(8,128)S(1)}, u32[]{:S(2)}, u32[]{:S(2)}) collective-permute-start(f32[16,32]{1,0:T(8,128)S(1)} %convert_element_type.7.mask_ref), channel_id=1, source_target_pairs={{0,8},{8,0},{16,24},{24,16},{32,40},{40,32},{48,56},{56,48},{64,72... | collective-permute-start | bytes 6152 | tf_op jit(solution)/shard_map/ppermute | solution.py:267
  14.1 15.3 %collective-permute-start.6 = (f32[4,8,384]{2,1,0:T(8,128)S(1)}, f32[4,8,384]{2,1,0:T(8,128)S(1)}, u32[]{:S(2)}, u32[]{:S(2)}) collective-permute-start(f32[4,8,384]{2,1,0:T(8,128)S(1)} %pad_maximum_fusion.1.cols_ref), channel_id=1, source_target_pairs={{0,128},{8,136},{16,144},{24,152},{32,160},{40,168},{48,176},{56,1... | collective-permute-start | bytes 147464 | tf_op jit(solution)/shard_map/ppermute | solution.py:267
  37.6 16.8 %all-to-all-start = ((f32[16,48,128]{2,1,0:T(8,128)}), f32[16,48,128]{2,1,0:T(8,128)S(1)}, u32[]{:S(2)}, u32[]{:S(2)}) async-start(f32[16,48,128]{2,1,0:T(8,128)} %shard_map.60), calls=%async_computation | async-start | bytes 786432 | tf_op jit(solution)/shard_map/all_to_all | solution.py:294
  41.7 16.9 %collective-permute-start.8 = (f32[2,8,128]{2,1,0:T(8,128)S(1)}, f32[2,8,128]{2,1,0:T(8,128)S(1)}, u32[]{:S(2)}, u32[]{:S(2)}) collective-permute-start(f32[2,8,128]{2,1,0:T(8,128)S(1)} %pad_maximum_fusion.5), channel_id=1, source_target_pairs={{0,1},{1,0},{2,3},{3,2},{4,5},{5,4},{6,7},{7,6},{8,9},{9,8},{10,11... | collective-permute-start | bytes 24584 | tf_op jit(solution)/shard_map/ppermute | solution.py:268
  55.1 13.1 %all-to-all-start.1 = ((f32[8,48,128]{2,1,0:T(8,128)}), f32[8,48,128]{2,1,0:T(8,128)S(1)}, u32[]{:S(2)}, u32[]{:S(2)}) async-start(f32[8,48,128]{2,1,0:T(8,128)} %broadcast_in_dim.25), calls=%async_computation.1 | async-start | bytes 393216 | tf_op jit(solution)/shard_map/all_to_all | solution.py:306
  58.6 5.3 %collective-permute-start.9 = (f32[4,8,128]{2,1,0:T(8,128)S(1)}, f32[4,8,128]{2,1,0:T(8,128)S(1)}, u32[]{:S(2)}, u32[]{:S(2)}) collective-permute-start(f32[4,8,128]{2,1,0:T(8,128)S(1)} %pad_maximum_fusion.4), channel_id=1, source_target_pairs={{0,2},{1,3},{2,0},{3,1},{4,6},{5,7},{6,4},{7,5},{8,10},{9,11},{10,... | collective-permute-start | bytes 49160 | tf_op jit(solution)/shard_map/ppermute | solution.py:268
  63.9 5.4 %collective-permute-start.10 = (f32[8,8,128]{2,1,0:T(8,128)S(1)}, f32[8,8,128]{2,1,0:T(8,128)S(1)}, u32[]{:S(2)}, u32[]{:S(2)}) collective-permute-start(f32[8,8,128]{2,1,0:T(8,128)S(1)} %pad_maximum_fusion.2), channel_id=1, source_target_pairs={{0,4},{1,5},{2,6},{3,7},{4,0},{5,1},{6,2},{7,3},{8,12},{9,13},{10,... | collective-permute-start | bytes 98312 | tf_op jit(solution)/shard_map/ppermute | solution.py:268
  68.2 13.1 %collective-permute-start.7 = (f32[8,48,128]{2,1,0:T(8,128)S(1)}, f32[8,48,128]{2,1,0:T(8,128)S(1)}, u32[]{:S(2)}, u32[]{:S(2)}) collective-permute-start(f32[8,48,128]{2,1,0:T(8,128)S(1)} %all-to-all-done.1.field_ref), channel_id=1, source_target_pairs={{0,8},{8,0},{16,24},{24,16},{32,40},{40,32},{48,56},{56,48},{64,72... | collective-permute-start | bytes 589832 | tf_op jit(solution)/shard_map/ppermute | solution.py:267
  114.8 1.4 %collective-permute-start.11 = (f32[8,48,128]{2,1,0:T(8,128)S(1)}, f32[8,48,128]{2,1,0:T(8,128)S(1)}, u32[]{:S(2)}, u32[]{:S(2)}) collective-permute-start(f32[8,48,128]{2,1,0:T(8,128)S(1)} %all_to_all.26.field_ref), channel_id=1, source_target_pairs={{0,8},{8,0},{16,24},{24,16},{32,40},{40,32},{48,56},{56,48},{64,72... | collective-permute-start | bytes 589832 | tf_op jit(solution)/shard_map/ppermute | solution.py:267
